TPU v7x, 32 devices: a whole 2x2x4 slice. The times are simulated.
32 devices in a mesh: dp: 8 (over y, x, core), mp: 4 (over z).
Axes of the slice: x: 2, y: 2, z: 4, core: 2. Of those that a mesh axis runs over, the one named last changes fastest.
Arguments:
- tokens: bfloat16 [16384, 2048], P(('dp', 'mp')), may hold values from -6 to 6
- segment_ids: int32 [16384], P('dp'), may hold values from 0 to 1, as said below
- grad_out: bfloat16 [16384, 2048], P(('dp', 'mp')), may hold values from -6 to 6
- attn_gain: bfloat16 [2048], replicated, may hold values from 0.5 to 1.5
- w_query: bfloat16 [2048, 2048], P(None, 'mp'), may hold values from -0.125 to 0.125
- w_key: bfloat16 [2048, 512], P(None, 'mp'), may hold values from -0.125 to 0.125
- w_value: bfloat16 [2048, 512], P(None, 'mp'), may hold values from -0.125 to 0.125
- w_output: bfloat16 [2048, 2048], P('mp'), may hold values from -0.75 to 0.75
- ffn_gain: bfloat16 [2048], replicated, may hold values from 0.5 to 1.5
- w_gate: bfloat16 [2048, 8192], P(None, 'mp'), may hold values from -0.125 to 0.125
- w_up: bfloat16 [2048, 8192], P(None, 'mp'), may hold values from -0.125 to 0.125
- w_down: bfloat16 [8192, 2048], P('mp'), may hold values from -0.0625 to 0.0625
Outputs:
- layer_out: bfloat16 [16384, 2048], P(('dp', 'mp'))
- grad_tokens: bfloat16 [16384, 2048], P(('dp', 'mp'))
- grad_attn_gain: float32 [2048], replicated
- grad_w_query: float32 [2048, 2048], P('dp', 'mp')
- grad_w_key: float32 [2048, 512], P('dp', 'mp')
- grad_w_value: float32 [2048, 512], P('dp', 'mp')
- grad_w_output: float32 [2048, 2048], P('mp', 'dp')
- grad_ffn_gain: float32 [2048], replicated
- grad_w_gate: float32 [2048, 8192], P('dp', 'mp')
- grad_w_up: float32 [2048, 8192], P('dp', 'mp')
- grad_w_down: float32 [8192, 2048], P('mp', 'dp')
Inputs may be any that keep to these rules, and one draw needn't show every extreme that they name: `segment_ids`: each block of 2048 rows (one index of dp) holds whole sequences numbered from 0 in order; every length is a multiple of 1024; in one block a single sequence fills all 2048 rows, in another every sequence has 1024 rows.
All inputs are finite; a program needn't handle non-finite values.
Results may differ from a plain program's by a relative error of at most 0.02.
Values may be sent and summed in bfloat16 or wider, within the bound.
No kernel may reach another device: no remote copies, remote signals or barrier semaphores. Data moves between devices by JAX's collectives and lax.ppermute only.
A program may use at most 320 MiB of HBM per device.

v0:
```python
import math

import jax
import jax.numpy as jnp
from jax import lax
from jax.sharding import PartitionSpec as P

HD = 64


norm_eps = 1e-05
score_scale = 0.125


def rope_table(places):
    half_dim = HD // 2
    freq_index = jnp.arange(half_dim, dtype=jnp.float32)
    base_freq = jnp.power(jnp.float32(500000.0), -2.0 * freq_index / HD)
    wave_len = 2.0 * math.pi / base_freq
    smooth = (8192.0 / wave_len - 1.0) / 3.0
    blended = (1.0 - smooth) * base_freq / 32.0 + smooth * base_freq
    frequency = jnp.where(
        wave_len < 2048.0, base_freq, jnp.where(wave_len > 8192.0, base_freq / 32.0, blended)
    )
    angles = places[:, None] * frequency[None, :]
    cos_table = jnp.concatenate([jnp.cos(angles), jnp.cos(angles)], axis=-1)
    sin_table = jnp.concatenate([jnp.sin(angles), jnp.sin(angles)], axis=-1)
    return (cos_table, sin_table)


def places_of(segment):
    row_count = segment.shape[0]
    row_index = jnp.arange(row_count, dtype=jnp.int32)
    new_start = jnp.concatenate([jnp.ones((1,), dtype=jnp.bool_), segment[1:] != segment[:-1]])
    first_row = lax.cummax(jnp.where(new_start, row_index, 0), axis=0)
    return ((row_index - first_row).astype(jnp.float32), row_index)


def rotate(values, cos_table, sin_table):
    half_dim = values.shape[-1] // 2
    turned = jnp.concatenate([-values[..., half_dim:], values[..., :half_dim]], axis=-1)
    return values * cos_table[:, None, :] + turned * sin_table[:, None, :]


def norm_back(values, inv_root, gain_vec, d_norm):
    scaled = d_norm * gain_vec
    inner_sum = jnp.mean(scaled * values, axis=-1, keepdims=True)
    d_values = inv_root * scaled - values * (inv_root * inv_root * inv_root) * inner_sum
    return (d_values, jnp.sum(d_norm * values * inv_root, axis=0))


def per_device(
    tokens,
    segment_ids,
    grad_out,
    attn_gain,
    w_query,
    w_key,
    w_value,
    w_output,
    ffn_gain,
    w_gate,
    w_up,
    w_down,
):
    row_data = tokens.astype(jnp.float32)
    gain_one = attn_gain.astype(jnp.float32)
    gain_two = ffn_gain.astype(jnp.float32)
    row_count = segment_ids.shape[0]
    heads_local = w_query.shape[1] // HD
    groups_local = w_key.shape[1] // HD
    per_group = heads_local // groups_local
    block_rows = min(512, row_count)
    block_count = row_count // block_rows
    inv_one = lax.rsqrt(jnp.mean(row_data * row_data, axis=-1, keepdims=True) + norm_eps)
    normed_one = (row_data * inv_one * gain_one).astype(jnp.bfloat16)
    full_one = lax.all_gather(normed_one, "mp", axis=0, tiled=True)
    query_raw = jnp.dot(full_one, w_query, preferred_element_type=jnp.float32)
    key_raw = jnp.dot(full_one, w_key, preferred_element_type=jnp.float32)
    value_low = (
        jnp.dot(full_one, w_value, preferred_element_type=jnp.float32)
        .astype(jnp.bfloat16)
        .reshape(row_count, groups_local, HD)
    )
    places, row_index = places_of(segment_ids)
    cos_table, sin_table = rope_table(places)
    query_rot = rotate(query_raw.reshape(row_count, heads_local, HD), cos_table, sin_table).astype(
        jnp.bfloat16
    )
    key_rot = rotate(key_raw.reshape(row_count, groups_local, HD), cos_table, sin_table).astype(
        jnp.bfloat16
    )
    query_blocks = query_rot.reshape(block_count, block_rows, groups_local, per_group, HD)
    seg_blocks = segment_ids.reshape(block_count, block_rows)
    index_blocks = row_index.reshape(block_count, block_rows)

    def block_scores(query_block, seg_block, index_block):
        scores = (
            jnp.einsum("qgrd,kgd->grqk", query_block, key_rot, preferred_element_type=jnp.float32)
            * score_scale
        )
        allowed = (seg_block[:, None] == segment_ids[None, :]) & (
            index_block[:, None] >= row_index[None, :]
        )
        return jnp.where(allowed, scores, -1e30)

    def attend(pieces):
        query_block, seg_block, index_block = pieces
        scores = block_scores(query_block, seg_block, index_block)
        row_max = jnp.max(scores, axis=-1, keepdims=True)
        raised = jnp.exp(scores - row_max)
        row_sum = jnp.sum(raised, axis=-1, keepdims=True)
        chance = (raised / row_sum).astype(jnp.bfloat16)
        attended = jnp.einsum(
            "grqk,kgd->qgrd", chance, value_low, preferred_element_type=jnp.float32
        )
        return (
            attended.reshape(block_rows, heads_local * HD).astype(jnp.bfloat16),
            row_max,
            row_sum,
        )

    attn_blocks, max_blocks, sum_blocks = lax.map(attend, (query_blocks, seg_blocks, index_blocks))
    attn_low = attn_blocks.reshape(row_count, heads_local * HD)
    piece = attn_low
    attn_sum = lax.psum_scatter(
        jnp.dot(piece, w_output, preferred_element_type=jnp.float32).astype(jnp.bfloat16),
        "mp",
        scatter_dimension=0,
        tiled=True,
    ).astype(jnp.float32)
    mid_rows = row_data + attn_sum
    inv_two = lax.rsqrt(jnp.mean(mid_rows * mid_rows, axis=-1, keepdims=True) + norm_eps)
    normed_two = (mid_rows * inv_two * gain_two).astype(jnp.bfloat16)
    full_two = lax.all_gather(normed_two, "mp", axis=0, tiled=True)
    gate_act = jnp.dot(full_two, w_gate, preferred_element_type=jnp.float32)
    up_act = jnp.dot(full_two, w_up, preferred_element_type=jnp.float32)
    gate_sigmoid = jax.nn.sigmoid(gate_act)
    hidden = (gate_act * gate_sigmoid * up_act).astype(jnp.bfloat16)
    piece = hidden
    ffn_sum = lax.psum_scatter(
        jnp.dot(piece, w_down, preferred_element_type=jnp.float32).astype(jnp.bfloat16),
        "mp",
        scatter_dimension=0,
        tiled=True,
    ).astype(jnp.float32)
    layer_out = (mid_rows + ffn_sum).astype(jnp.bfloat16)
    back_rows = grad_out.astype(jnp.float32)
    back_full = lax.all_gather(grad_out, "mp", axis=0, tiled=True)
    d_hidden = jnp.dot(back_full, w_down.T, preferred_element_type=jnp.float32)
    grad_down = jnp.dot(hidden.T, back_full, preferred_element_type=jnp.float32)
    d_gate = (d_hidden * up_act * gate_sigmoid * (1.0 + gate_act * (1.0 - gate_sigmoid))).astype(
        jnp.bfloat16
    )
    d_up = (d_hidden * gate_act * gate_sigmoid).astype(jnp.bfloat16)
    grad_gate = jnp.dot(full_two.T, d_gate, preferred_element_type=jnp.float32)
    grad_up = jnp.dot(full_two.T, d_up, preferred_element_type=jnp.float32)
    d_norm_two = lax.psum_scatter(
        (
            jnp.dot(d_gate, w_gate.T, preferred_element_type=jnp.float32)
            + jnp.dot(d_up, w_up.T, preferred_element_type=jnp.float32)
        ).astype(jnp.bfloat16),
        "mp",
        scatter_dimension=0,
        tiled=True,
    ).astype(jnp.float32)
    d_from_two, gain_two_part = norm_back(mid_rows, inv_two, gain_two, d_norm_two)
    d_mid = back_rows + d_from_two
    d_attn_full = lax.all_gather(d_mid.astype(jnp.bfloat16), "mp", axis=0, tiled=True)
    grad_output = jnp.dot(attn_low.T, d_attn_full, preferred_element_type=jnp.float32)
    d_attended = jnp.dot(d_attn_full, w_output.T, preferred_element_type=jnp.float32).astype(
        jnp.bfloat16
    )
    d_attended = d_attended.reshape(block_count, block_rows, groups_local, per_group, HD)

    def attend_back(carried, pieces):
        key_sum, value_sum = carried
        query_block, seg_block, index_block, max_block, sum_block, grad_block = pieces
        scores = block_scores(query_block, seg_block, index_block)
        chance = jnp.exp(scores - max_block) / sum_block
        d_chance = jnp.einsum(
            "qgrd,kgd->grqk", grad_block, value_low, preferred_element_type=jnp.float32
        )
        d_scores = (
            chance * (d_chance - jnp.sum(d_chance * chance, axis=-1, keepdims=True))
        ).astype(jnp.bfloat16)
        value_sum = value_sum + jnp.einsum(
            "grqk,qgrd->kgd",
            chance.astype(jnp.bfloat16),
            grad_block,
            preferred_element_type=jnp.float32,
        )
        key_sum = (
            key_sum
            + jnp.einsum(
                "grqk,qgrd->kgd", d_scores, query_block, preferred_element_type=jnp.float32
            )
            * score_scale
        )
        d_query = (
            jnp.einsum("grqk,kgd->qgrd", d_scores, key_rot, preferred_element_type=jnp.float32)
            * score_scale
        )
        return ((key_sum, value_sum), d_query)

    zero_heads = jnp.zeros((row_count, groups_local, HD), jnp.float32)
    (key_sum, value_sum), d_query = lax.scan(
        attend_back,
        (zero_heads, zero_heads),
        (query_blocks, seg_blocks, index_blocks, max_blocks, sum_blocks, d_attended),
    )
    d_query_raw = (
        rotate(d_query.reshape(row_count, heads_local, HD), cos_table, -sin_table)
        .astype(jnp.bfloat16)
        .reshape(row_count, heads_local * HD)
    )
    d_key_raw = (
        rotate(key_sum, cos_table, -sin_table)
        .astype(jnp.bfloat16)
        .reshape(row_count, groups_local * HD)
    )
    d_value = value_sum.astype(jnp.bfloat16).reshape(row_count, groups_local * HD)
    grad_query = jnp.dot(full_one.T, d_query_raw, preferred_element_type=jnp.float32)
    grad_key = jnp.dot(full_one.T, d_key_raw, preferred_element_type=jnp.float32)
    grad_value = jnp.dot(full_one.T, d_value, preferred_element_type=jnp.float32)
    summed = jnp.dot(d_query_raw, w_query.T, preferred_element_type=jnp.float32)
    summed = summed + jnp.dot(d_key_raw, w_key.T, preferred_element_type=jnp.float32)
    d_norm_one = lax.psum_scatter(
        (summed + jnp.dot(d_value, w_value.T, preferred_element_type=jnp.float32)).astype(
            jnp.bfloat16
        ),
        "mp",
        scatter_dimension=0,
        tiled=True,
    ).astype(jnp.float32)
    d_from_one, gain_one_part = norm_back(row_data, inv_one, gain_one, d_norm_one)
    grad_tokens = (d_mid + d_from_one).astype(jnp.bfloat16)
    grad_gain_one, grad_gain_two = lax.psum((gain_one_part, gain_two_part), ("dp", "mp"))
    (
        grad_query_sum,
        grad_key_sum,
        grad_value_sum,
        grad_output_sum,
        grad_gate_sum,
        grad_up_sum,
        grad_down_sum,
    ) = (
        lax.psum_scatter(
            grad_query.astype(jnp.bfloat16), "dp", scatter_dimension=0, tiled=True
        ).astype(jnp.float32),
        lax.psum_scatter(
            grad_key.astype(jnp.bfloat16), "dp", scatter_dimension=0, tiled=True
        ).astype(jnp.float32),
        lax.psum_scatter(
            grad_value.astype(jnp.bfloat16), "dp", scatter_dimension=0, tiled=True
        ).astype(jnp.float32),
        lax.psum_scatter(
            grad_output.astype(jnp.bfloat16), "dp", scatter_dimension=1, tiled=True
        ).astype(jnp.float32),
        lax.psum_scatter(
            grad_gate.astype(jnp.bfloat16), "dp", scatter_dimension=0, tiled=True
        ).astype(jnp.float32),
        lax.psum_scatter(
            grad_up.astype(jnp.bfloat16), "dp", scatter_dimension=0, tiled=True
        ).astype(jnp.float32),
        lax.psum_scatter(
            grad_down.astype(jnp.bfloat16), "dp", scatter_dimension=1, tiled=True
        ).astype(jnp.float32),
    )
    return (
        layer_out,
        grad_tokens,
        grad_gain_one,
        grad_query_sum,
        grad_key_sum,
        grad_value_sum,
        grad_output_sum,
        grad_gain_two,
        grad_gate_sum,
        grad_up_sum,
        grad_down_sum,
    )


def solution(mesh):
    placed = (
        P(("dp", "mp"), None),
        P("dp"),
        P(("dp", "mp"), None),
        P(),
        P(None, "mp"),
        P(None, "mp"),
        P(None, "mp"),
        P("mp", None),
        P(),
        P(None, "mp"),
        P(None, "mp"),
        P("mp", None),
    )
    return jax.shard_map(
        per_device,
        mesh=mesh,
        in_specs=placed,
        out_specs=(
            P(("dp", "mp"), None),
            P(("dp", "mp"), None),
            P(),
            P("dp", "mp"),
            P("dp", "mp"),
            P("dp", "mp"),
            P("mp", "dp"),
            P(),
            P("dp", "mp"),
            P("dp", "mp"),
            P("mp", "dp"),
        ),
        check_vma=False,
    )
```

profile of v0, /device:TPU:0, one launch (start us, length us, event | category | flops | bytes accessed | tf_op | source)
XLA Modules:
  0.0 2268.9 jit_solution(17204468212221466734)
XLA Ops:
  21.5 145.8 %all-gather.5.cloned.1.call-done = bf16[2048,2048]{1,0:T(8,128)(2,1)} async-done(((bf16[512,2048]{1,0:T(8,128)(2,1)}), bf16[2048,2048]{1,0:T(8,128)(2,1)}) %all-gather.5.cloned.1.call-update) | async-done | bytes 8388624 | tf_op jit(solution)/shard_map/all_gather | solution.py:77
  211.4 194.2 %while.30 = (s32[]{:T(128)}, bf16[4,512,512]{2,1,0:T(8,128)(2,1)}, f32[4,2,4,512,1]{3,2,1,4,0:T(4,128)}, f32[4,2,4,512,1]{3,2,1,4,0:T(4,128)}, s32[4,512]{1,0:T(...) while((s32[]{:T(128)}, bf16[4,512,512]{2,1,0:T(8,128)(2,1)}, ...), condition=%wide.region_6.7_spmd.clone, body=%wide.region_3.6_spmd.clone.sunk | while | flops 2251546624 | bytes 109219968 | solution.py:123
  212.6 14.8 bitcast_reduce_fusion.2
  227.5 15.0 fusion.153
  242.5 14.8 fusion.154
  261.2 14.8 bitcast_reduce_fusion.2
  276.0 15.0 fusion.153
  291.0 14.8 fusion.154
  309.8 14.8 bitcast_reduce_fusion.2
  324.6 15.0 fusion.153
  339.6 14.8 fusion.154
  358.3 14.8 bitcast_reduce_fusion.2
  373.1 15.0 fusion.153
  388.1 14.8 fusion.154
  405.7 8.6 convolution_convert_fusion.4
  415.0 142.3 %reduce-scatter.12.cloned.1.call-done = bf16[512,2048]{1,0:T(8,128)(2,1)} async-done(((bf16[2048,2048]{1,0:T(8,128)(2,1)}), bf16[512,2048]{1,0:T(8,128)(2,1)}) %reduce-scatter.12.cloned.1.call-update) | async-done | bytes 2097168 | tf_op jit(solution)/shard_map/reduce_scatter | solution.py:126
  564.6 149.8 %all-gather.7.cloned.1.call-done = bf16[2048,2048]{1,0:T(8,128)(2,1)} async-done(((bf16[512,2048]{1,0:T(8,128)(2,1)}), bf16[2048,2048]{1,0:T(8,128)(2,1)}) %all-gather.7.cloned.1.call-update) | async-done | bytes 8388624 | tf_op jit(solution)/shard_map/all_gather | solution.py:135
  714.3 24.6 %fusion.84 = f32[2048,2048]{1,0:T(8,128)} fusion(bf16[2048,2048]{1,0:T(8,128)(2,1)} %all-gather.7.cloned.1.call-done, bf16[2048,2048]{1,0:T(8,128)(2,1)} %param.26), kind=kOutput, calls=%fused_computation.161 | convolution fusion | flops 17179869184 | bytes 33554432 | tf_op jit(solution)/shard_map/dot_general | solution.py:137
  738.9 21.8 fusion.83
  760.7 102.9 %all-gather.9.cloned.1.call-done = bf16[2048,2048]{1,0:T(8,128)(2,1)} async-done(((bf16[512,2048]{1,0:T(8,128)(2,1)}), bf16[2048,2048]{1,0:T(8,128)(2,1)}) %all-gather.9.cloned.1.call-update) | async-done | bytes 8388624 | tf_op jit(solution)/shard_map/all_gather | solution.py:149
  863.6 36.8 %multiply_convert_fusion = (bf16[2048,2048]{1,0:T(8,128)(2,1)}, bf16[2048,2048]{1,0:T(8,128)(2,1)}, bf16[2048,2048]{1,0:T(8,128)(2,1)}) fusion(f32[2048,2048]{1,0:T(8,128)} %fusion.83, f32[2048,2048]{1,0:T(8,128)} %fusion.84, bf16[2048,2048]{1,0:T(8,128)(2,1)} %all-gather.9.cloned.1.call-done, bf16[2048,2048]{1,0:T(8,128)(2,1)} %param.27), kind=kOutput, calls=%fused_computation.67 | convolution fusion | flops 17246978048 | bytes 75497472 | tf_op jit(solution)/shard_map/dot_general | solution.py:150
  900.3 24.3 %fusion.85 = f32[2048,2048]{1,0:T(8,128)} fusion(bf16[2048,2048]{1,0:T(8,128)(2,1)} %get-tuple-element.315, bf16[2048,2048]{1,0:T(8,128)(2,1)} %param.25), kind=kOutput, calls=%fused_computation.162 | convolution fusion | flops 17179869184 | bytes 33554432 | tf_op jit(solution)/shard_map/dot_general | solution.py:160
  924.6 25.6 %add_convert_fusion.1 = bf16[2048,2048]{1,0:T(8,128)(2,1)} fusion(f32[2048,2048]{1,0:T(8,128)} %fusion.85, bf16[2048,2048]{1,0:T(8,128)(2,1)} %get-tuple-element.314, bf16[2048,2048]{1,0:T(8,128)(2,1)} %param.26), kind=kOutput, calls=%fused_computation.66 | convolution fusion | flops 17188257792 | bytes 41943040 | tf_op jit(solution)/shard_map/dot_general | solution.py:161
  950.4 142.9 %reduce-scatter.16.cloned.1.call-done = bf16[512,2048]{1,0:T(8,128)(2,1)} async-done(((bf16[2048,2048]{1,0:T(8,128)(2,1)}), bf16[512,2048]{1,0:T(8,128)(2,1)}) %reduce-scatter.16.cloned.1.call-update) | async-done | bytes 2097168 | tf_op jit(solution)/shard_map/reduce_scatter | solution.py:158
  1103.2 23.7 %convolution_convert_fusion = bf16[2048,2048]{1,0:T(8,128)(2,1)} fusion(bf16[2048,2048]{1,0:T(8,128)(2,1)} %get-tuple-element.316, bf16[2048,2048]{1,0:T(8,128)(2,1)} %all-gather.9.cloned.1.call-done), kind=kOutput, calls=%fused_computation.77 | convolution fusion | flops 17184063488 | bytes 25165824 | tf_op jit(solution)/shard_map/dot_general | solution.py:151
  1127.0 24.2 %convolution_convert_fusion.1 = bf16[2048,2048]{1,0:T(8,128)(2,1)} fusion(bf16[2048,2048]{1,0:T(8,128)(2,1)} %all-gather.7.cloned.1.call-done, bf16[2048,2048]{1,0:T(8,128)(2,1)} %get-tuple-element.314), kind=kOutput, calls=%fused_computation.78 | convolution fusion | flops 17184063488 | bytes 25165824 | tf_op jit(solution)/shard_map/dot_general | solution.py:157
  1151.3 23.8 %convolution_convert_fusion.2 = bf16[2048,2048]{1,0:T(8,128)(2,1)} fusion(bf16[2048,2048]{1,0:T(8,128)(2,1)} %all-gather.7.cloned.1.call-done, bf16[2048,2048]{1,0:T(8,128)(2,1)} %get-tuple-element.315), kind=kOutput, calls=%fused_computation.79 | convolution fusion | flops 17184063488 | bytes 25165824 | tf_op jit(solution)/shard_map/dot_general | solution.py:156
  1175.2 78.3 %all-gather.11.cloned.1.call-done = bf16[2048,2048]{1,0:T(8,128)(2,1)} async-done(((bf16[512,2048]{1,0:T(8,128)(2,1)}), bf16[2048,2048]{1,0:T(8,128)(2,1)}) %all-gather.11.cloned.1.call-update) | async-done | bytes 8388624 | tf_op jit(solution)/shard_map/all_gather | solution.py:169
  1253.5 9.1 convolution_convert_fusion.7
  1277.4 512.4 %while.31 = (s32[]{:T(128)}, f32[2048,2,64]{0,2,1:T(8,128)S(1)}, f32[2048,2,64]{0,2,1:T(8,128)S(1)}, f32[4,512,2,4,64]{1,0,4,3,2:T(4,128)}, bf16[4,512,2,4,64]{1...) while((s32[]{:T(128)}, f32[2048,2,64]{0,2,1:T(8,128)S(1)}, ...), condition=%wide.region_14.15_spmd.clone, body=%wide.region_12.14_spmd.clone.sunk | while | flops 5457309696 | bytes 338317600 | solution.py:207
  1280.3 18.1 fusion.163
  1298.4 26.0 %fusion.165 = (f32[2,4,512]{2,1,0:T(4,128)S(1)}, f32[2,4,512,2048]{3,2,1,0:T(8,128)}) fusion(f32[2,512,4,2048]{3,1,2,0:T(8,128)} %fusion.163, f32[2,4,512]{2,1,0:T(4,128)S(1)} %get-tuple-element.494, f32[2,4,512]{2,1,0:T(4,128)S(1)} %get-tuple-element.495, bf16[2048,2,64]{0,2,1:T(8,128)(2,1)S(1)} %copy-done.10, ...), kind=kOutput, calls=%fused_computation.27.clone.1 | convolution fusion | flops 1124069376 | bytes 69255168 | tf_op jit(solution)/shard_map/while/body/eval_jaxpr/qgrd,kgd->grqk/dot_general | solution.py:99
  1324.4 30.7 %fusion.166 = bf16[2,4,512,2048]{3,2,1,0:T(8,128)(2,1)} fusion(f32[2,4,512,2048]{3,2,1,0:T(8,128)} %get-tuple-element.498, f32[2,512,4,2048]{3,1,2,0:T(8,128)} %fusion.163, f32[2,4,512]{2,1,0:T(4,128)S(1)} %get-tuple-element.499), kind=kLoop, calls=%fused_computation.29.clone.1 | loop fusion | flops 25165824 | bytes 83902464 | tf_op jit(solution)/shard_map/while/body/eval_jaxpr/convert_element_type | solution.py:186
  1355.1 14.7 fusion.168
  1369.8 9.5 fusion.167
  1388.2 21.1 dynamic_update_slice.27
  1412.0 18.8 fusion.163
  1430.9 26.0 %fusion.165 = (f32[2,4,512]{2,1,0:T(4,128)S(1)}, f32[2,4,512,2048]{3,2,1,0:T(8,128)}) fusion(f32[2,512,4,2048]{3,1,2,0:T(8,128)} %fusion.163, f32[2,4,512]{2,1,0:T(4,128)S(1)} %get-tuple-element.494, f32[2,4,512]{2,1,0:T(4,128)S(1)} %get-tuple-element.495, bf16[2048,2,64]{0,2,1:T(8,128)(2,1)S(1)} %copy-done.10, ...), kind=kOutput, calls=%fused_computation.27.clone.1 | convolution fusion | flops 1124069376 | bytes 69255168 | tf_op jit(solution)/shard_map/while/body/eval_jaxpr/qgrd,kgd->grqk/dot_general | solution.py:99
  1456.9 28.0 %fusion.166 = bf16[2,4,512,2048]{3,2,1,0:T(8,128)(2,1)} fusion(f32[2,4,512,2048]{3,2,1,0:T(8,128)} %get-tuple-element.498, f32[2,512,4,2048]{3,1,2,0:T(8,128)} %fusion.163, f32[2,4,512]{2,1,0:T(4,128)S(1)} %get-tuple-element.499), kind=kLoop, calls=%fused_computation.29.clone.1 | loop fusion | flops 25165824 | bytes 83902464 | tf_op jit(solution)/shard_map/while/body/eval_jaxpr/convert_element_type | solution.py:186
  1484.9 13.9 fusion.168
  1498.9 9.2 fusion.167
  1516.8 21.1 dynamic_update_slice.27
  1540.6 16.9 fusion.163
  1557.4 25.8 %fusion.165 = (f32[2,4,512]{2,1,0:T(4,128)S(1)}, f32[2,4,512,2048]{3,2,1,0:T(8,128)}) fusion(f32[2,512,4,2048]{3,1,2,0:T(8,128)} %fusion.163, f32[2,4,512]{2,1,0:T(4,128)S(1)} %get-tuple-element.494, f32[2,4,512]{2,1,0:T(4,128)S(1)} %get-tuple-element.495, bf16[2048,2,64]{0,2,1:T(8,128)(2,1)S(1)} %copy-done.10, ...), kind=kOutput, calls=%fused_computation.27.clone.1 | convolution fusion | flops 1124069376 | bytes 69255168 | tf_op jit(solution)/shard_map/while/body/eval_jaxpr/qgrd,kgd->grqk/dot_general | solution.py:99
  1583.2 27.5 %fusion.166 = bf16[2,4,512,2048]{3,2,1,0:T(8,128)(2,1)} fusion(f32[2,4,512,2048]{3,2,1,0:T(8,128)} %get-tuple-element.498, f32[2,512,4,2048]{3,1,2,0:T(8,128)} %fusion.163, f32[2,4,512]{2,1,0:T(4,128)S(1)} %get-tuple-element.499), kind=kLoop, calls=%fused_computation.29.clone.1 | loop fusion | flops 25165824 | bytes 83902464 | tf_op jit(solution)/shard_map/while/body/eval_jaxpr/convert_element_type | solution.py:186
  1610.7 13.9 fusion.168
  1624.7 9.2 fusion.167
  1642.6 21.1 dynamic_update_slice.27
  1666.4 16.9 fusion.163
  1683.2 25.8 %fusion.165 = (f32[2,4,512]{2,1,0:T(4,128)S(1)}, f32[2,4,512,2048]{3,2,1,0:T(8,128)}) fusion(f32[2,512,4,2048]{3,1,2,0:T(8,128)} %fusion.163, f32[2,4,512]{2,1,0:T(4,128)S(1)} %get-tuple-element.494, f32[2,4,512]{2,1,0:T(4,128)S(1)} %get-tuple-element.495, bf16[2048,2,64]{0,2,1:T(8,128)(2,1)S(1)} %copy-done.10, ...), kind=kOutput, calls=%fused_computation.27.clone.1 | convolution fusion | flops 1124069376 | bytes 69255168 | tf_op jit(solution)/shard_map/while/body/eval_jaxpr/qgrd,kgd->grqk/dot_general | solution.py:99
  1709.0 27.5 %fusion.166 = bf16[2,4,512,2048]{3,2,1,0:T(8,128)(2,1)} fusion(f32[2,4,512,2048]{3,2,1,0:T(8,128)} %get-tuple-element.498, f32[2,512,4,2048]{3,1,2,0:T(8,128)} %fusion.163, f32[2,4,512]{2,1,0:T(4,128)S(1)} %get-tuple-element.499), kind=kLoop, calls=%fused_computation.29.clone.1 | loop fusion | flops 25165824 | bytes 83902464 | tf_op jit(solution)/shard_map/while/body/eval_jaxpr/convert_element_type | solution.py:186
  1736.5 13.9 fusion.168
  1750.4 9.2 fusion.167
  1768.4 21.1 dynamic_update_slice.27
  1805.8 10.0 convolution_convert_fusion.5
  1838.7 8.2 fusion.87
  1846.9 8.6 fusion.86
  1855.5 15.5 add_convert_fusion
  1871.0 23.6 %convolution_convert_fusion.3 = bf16[2048,2048]{1,0:T(8,128)(2,1)} fusion(bf16[2048,2048]{1,0:T(8,128)(2,1)} %get-tuple-element.316, bf16[2048,2048]{1,0:T(8,128)(2,1)} %param.27), kind=kOutput, calls=%fused_computation.80 | convolution fusion | flops 17184063488 | bytes 25165824 | tf_op jit(solution)/shard_map/dot_general | solution.py:142
  1915.7 43.2 %reduce-scatter.20.cloned.1.call-done = bf16[256,512]{1,0:T(8,128)(2,1)} async-done(((bf16[2048,512]{1,0:T(8,128)(2,1)}), bf16[256,512]{1,0:T(8,128)(2,1)}) %reduce-scatter.20.cloned.1.call-update) | async-done | bytes 262160 | tf_op jit(solution)/shard_map/reduce_scatter | solution.py:248
  1960.7 145.1 %reduce-scatter.18.cloned.1.call-done = bf16[512,2048]{1,0:T(8,128)(2,1)} async-done(((bf16[2048,2048]{1,0:T(8,128)(2,1)}), bf16[512,2048]{1,0:T(8,128)(2,1)}) %reduce-scatter.18.cloned.1.call-update) | async-done | bytes 2097168 | tf_op jit(solution)/shard_map/reduce_scatter | solution.py:228
  2109.0 46.0 %all-reduce = (f32[2048]{0:T(1024)}, f32[2048]{0:T(1024)}) all-reduce(f32[2048]{0:T(1024)S(1)} %get-tuple-element.254, f32[2048]{0:T(1024)S(1)} %copy-done.45), channel_id=1, replica_groups=mesh['dp'=8,'mp'=4] {'dp','mp'}, use_global_device_ids=true, to_apply=%region_18.19 | all-reduce | flops 4096 | bytes 32768 | tf_op jit(solution)/shard_map/psum | solution.py:238
  2155.0 99.2 %reduce-scatter.14.cloned.1.call-done = bf16[512,2048]{1,0:T(8,128)(2,1)} async-done(((bf16[2048,2048]{1,0:T(8,128)(2,1)}), bf16[512,2048]{1,0:T(8,128)(2,1)}) %reduce-scatter.14.cloned.1.call-update) | async-done | bytes 2097168 | tf_op jit(solution)/shard_map/reduce_scatter | solution.py:141
  2254.2 7.9 fusion.56
  (286 shorter events, 217.2 us)
Async XLA Ops:
  7.2 398.5 %copy-start = (bf16[512,2048]{1,0:T(8,128)(2,1)S(1)}, bf16[512,2048]{1,0:T(8,128)(2,1)}, u32[]{:S(2)}) copy-start(bf16[512,2048]{1,0:T(8,128)(2,1)} %param.23) | copy-start | bytes 6291460
  7.2 7.7 copy-start.31
  7.2 160.1 %all-gather.5.cloned.1.call-start = ((), (), s32[]{:S(2)}) async-start(), calls=%async_computation.11 | async-start | bytes 10485760 | tf_op jit(solution)/shard_map/all_gather | solution.py:77
  14.8 542.4 %reduce-scatter.12.cloned.1.call-start = ((), (), s32[]{:S(2)}) async-start(), calls=%async_computation.12 | async-start | bytes 10485760 | tf_op jit(solution)/shard_map/reduce_scatter | solution.py:126
  167.3 7.5 copy-start.7
  167.3 7.5 copy-start.53
  199.2 8.6 slice-start
  199.2 8.6 slice-start.1
  405.7 8.6 copy-start.38
  405.7 8.6 copy-start.39
  414.3 300.0 %all-gather.7.cloned.1.call-start = ((), (), s32[]{:S(2)}) async-start(), calls=%async_computation.13 | async-start | bytes 10485760 | tf_op jit(solution)/shard_map/all_gather | solution.py:135
  414.9 149.0 %copy-start.33 = (f32[2048]{0:T(1024)}, f32[2048]{0:T(1024)S(1)}, u32[]{:S(2)}) copy-start(f32[2048]{0:T(1024)S(1)} %convert_element_type.170) | copy-start | bytes 24580
  563.9 299.6 %all-gather.9.cloned.1.call-start = ((), (), s32[]{:S(2)}) async-start(), calls=%async_computation.15 | async-start | bytes 10485760 | tf_op jit(solution)/shard_map/all_gather | solution.py:149
  564.5 528.7 %reduce-scatter.16.cloned.1.call-start = ((), (), s32[]{:S(2)}) async-start(), calls=%async_computation.16 | async-start | bytes 10485760 | tf_op jit(solution)/shard_map/reduce_scatter | solution.py:158
  714.3 24.6 %copy-start.52 = (bf16[2048,2048]{1,0:T(8,128)(2,1)S(1)}, bf16[2048,2048]{1,0:T(8,128)(2,1)}, u32[]{:S(2)}) copy-start(bf16[2048,2048]{1,0:T(8,128)(2,1)} %all-gather.7.cloned.1.call-done) | copy-start | bytes 25165828
  950.3 143.0 %copy-start.34 = (f32[2048]{0:T(1024)S(1)}, f32[2048]{0:T(1024)}, u32[]{:S(2)}) copy-start(f32[2048]{0:T(1024)} %copy-done.33) | copy-start | bytes 24580
  950.3 143.0 %copy-start.41 = (f32[512]{0:T(512)S(1)}, f32[512]{0:T(512)}, u32[]{:S(2)}) copy-start(f32[512]{0:T(512)} %copy-done.40) | copy-start | bytes 6148
  950.3 148.7 %copy-start.46 = (f32[512]{0:T(512)S(1)}, f32[512]{0:T(512)}, u32[]{:S(2)}) copy-start(f32[512]{0:T(512)} %get-tuple-element.335) | copy-start | bytes 6148
  950.3 303.2 %all-gather.11.cloned.1.call-start = ((), (), s32[]{:S(2)}) async-start(), calls=%async_computation.17 | async-start | bytes 10485760 | tf_op jit(solution)/shard_map/all_gather | solution.py:169
  1093.3 5.8 copy-start.4
  1093.3 5.8 copy-start.9
  1103.1 791.6 %reduce-scatter.32.cloned.1.call-start = ((), (), s32[]{:S(2)}) async-start(), calls=%async_computation.25 | async-start | bytes 9437184 | tf_op jit(solution)/shard_map/reduce_scatter | solution.py:266
  1127.0 770.5 %reduce-scatter.30.cloned.1.call-start = ((), (), s32[]{:S(2)}) async-start(), calls=%async_computation.24 | async-start | bytes 9437184 | tf_op jit(solution)/shard_map/reduce_scatter | solution.py:263
  1151.2 749.2 %reduce-scatter.28.cloned.1.call-start = ((), (), s32[]{:S(2)}) async-start(), calls=%async_computation.23 | async-start | bytes 9437184 | tf_op jit(solution)/shard_map/reduce_scatter | solution.py:260
  1175.2 728.1 %reduce-scatter.24.cloned.1.call-start = ((), (), s32[]{:S(2)}) async-start(), calls=%async_computation.21 | async-start | bytes 589824 | tf_op jit(solution)/shard_map/reduce_scatter | solution.py:254
  1270.4 7.1 copy-start.6
  1270.4 7.1 copy-start.32
  1280.3 18.1 copy-start.10
  1369.8 11.2 copy-start.2
  1369.8 11.2 copy-start.11
  1412.0 18.8 copy-start.10
  1498.8 10.7 copy-start.2
  1498.8 10.7 copy-start.11
  1540.5 16.9 copy-start.10
  1624.6 10.7 copy-start.2
  1624.6 10.7 copy-start.11
  1666.3 16.9 copy-start.10
  1750.4 10.7 copy-start.2
  1750.4 10.7 copy-start.11
  1789.9 7.7 copy-start.21
  1790.9 6.8 copy-start.15
  1790.9 6.8 copy-start.17
  1797.6 107.1 %reduce-scatter.22.cloned.1.call-start = ((), (), s32[]{:S(2)}) async-start(), calls=%async_computation.20 | async-start | bytes 589824 | tf_op jit(solution)/shard_map/reduce_scatter | solution.py:251
  1799.0 6.8 copy-start.19
  1805.8 108.1 %reduce-scatter.26.cloned.1.call-start = ((), (), s32[]{:S(2)}) async-start(), calls=%async_computation.22 | async-start | bytes 2359296 | tf_op jit(solution)/shard_map/reduce_scatter | solution.py:257
  1815.9 143.0 %reduce-scatter.20.cloned.1.call-start = ((), (), s32[]{:S(2)}) async-start(), calls=%async_computation.19 | async-start | bytes 2359296 | tf_op jit(solution)/shard_map/reduce_scatter | solution.py:248
  1832.2 6.4 copy-start.20
  1832.2 6.4 copy-start.25
  1838.6 267.2 %reduce-scatter.18.cloned.1.call-start = ((), (), s32[]{:S(2)}) async-start(), calls=%async_computation.18 | async-start | bytes 10485760 | tf_op jit(solution)/shard_map/reduce_scatter | solution.py:228
  1838.6 8.2 copy-start.30
  1838.6 8.2 copy-start.54
  1846.8 8.6 copy-start.22
  1846.8 8.6 copy-start.24
  1871.0 383.2 %reduce-scatter.14.cloned.1.call-start = ((), (), s32[]{:S(2)}) async-start(), calls=%async_computation.14 | async-start | bytes 10485760 | tf_op jit(solution)/shard_map/reduce_scatter | solution.py:141
  1897.4 208.4 %copy-start.5 = (bf16[512,2048]{1,0:T(8,128)(2,1)S(1)}, bf16[512,2048]{1,0:T(8,128)(2,1)}, u32[]{:S(2)}) copy-start(bf16[512,2048]{1,0:T(8,128)(2,1)} %param.16) | copy-start | bytes 6291460
  1897.4 208.4 %copy-start.37 = (f32[2048]{0:T(1024)S(1)}, f32[2048]{0:T(1024)}, u32[]{:S(2)}) copy-start(f32[2048]{0:T(1024)} %copy-done.36) | copy-start | bytes 24580
  1897.4 208.4 %copy-start.44 = (f32[512]{0:T(512)S(1)}, f32[512]{0:T(512)}, u32[]{:S(2)}) copy-start(f32[512]{0:T(512)} %copy-done.43) | copy-start | bytes 6148
  1900.4 208.6 %copy-start.45 = (f32[2048]{0:T(1024)S(1)}, f32[2048]{0:T(1024)}, u32[]{:S(2)}) copy-start(f32[2048]{0:T(1024)} %get-tuple-element.252) | copy-start | bytes 24580
  1900.4 353.8 %copy-start.35 = (f32[2048]{0:T(1024)S(1)}, f32[2048]{0:T(1024)}, u32[]{:S(2)}) copy-start(f32[2048]{0:T(1024)} %copy-done.33) | copy-start | bytes 24580
  1900.4 353.8 %copy-start.42 = (f32[512]{0:T(512)S(1)}, f32[512]{0:T(512)}, u32[]{:S(2)}) copy-start(f32[512]{0:T(512)} %copy-done.40) | copy-start | bytes 6148
  1900.4 353.8 %copy-start.47 = (f32[512]{0:T(512)S(1)}, f32[512]{0:T(512)}, u32[]{:S(2)}) copy-start(f32[512]{0:T(512)} %get-tuple-element.335) | copy-start | bytes 6148
  1900.4 353.8 %copy-start.49 = (f32[512]{0:T(512)S(1)}, f32[512]{0:T(512)}, u32[]{:S(2)}) copy-start(f32[512]{0:T(512)} %copy-done.48) | copy-start | bytes 6148
  1900.4 353.8 %copy-start.50 = (f32[512]{0:T(512)S(1)}, f32[512]{0:T(512)}, u32[]{:S(2)}) copy-start(f32[512]{0:T(512)} %get-tuple-element.333) | copy-start | bytes 6148
  2254.2 7.9 copy-start.1
  (19 other events, 45.1 us)
Sparse Core Ops, SparseCore 0:
  14.9 152.3 all-gather.4
  414.4 142.7 reduce-scatter.11
  564.0 150.2 all-gather.6
  715.7 147.7 all-gather.8
  950.4 142.7 reduce-scatter.15
  1103.2 150.2 all-gather.10
  1257.0 69.4 reduce-scatter.31
  1329.9 71.5 reduce-scatter.29
  1404.9 71.5 reduce-scatter.27
  1797.8 34.0 reduce-scatter.23
  1834.9 34.1 reduce-scatter.21
  1872.8 41.1 reduce-scatter.25
  1917.8 41.0 reduce-scatter.19
  1961.1 144.6 reduce-scatter.17
  2108.0 146.1 reduce-scatter.13
where the time goes:
time: 2280 us; the launch traced here: 2270 us
  waiting for transfers between devices  1060 us (46%)
  matrix products  732 us (32%)
  other arithmetic  254 us (11%)
  local copies, waits for them, and re-layouts  164 us (7%)
  blocking collectives  46 us (2%)
    dot_general x8, matrix products, block_scores(): jnp.einsum('qgrd,kgd->grqk', query_block, key_rot, preferred_element_type...  163 us
    all_gather x1, waiting for transfers between devices, per_device(): full_two = lax.all_gather(normed_two, 'mp', axis=0, tiled=True)  150 us
    all_gather x1, waiting for transfers between devices, per_device(): full_one = lax.all_gather(normed_one, 'mp', axis=0, tiled=True)  146 us
    reduce_scatter x1, waiting for transfers between devices, per_device(): lax.psum_scatter((summed + jnp.dot(d_value, w_value.T, preferred_element_...  145 us
    reduce_scatter x1, waiting for transfers between devices, per_device(): lax.psum_scatter((jnp.dot(d_gate, w_gate.T, preferred_element_type=jnp.fl...  143 us
    reduce_scatter x1, waiting for transfers between devices, per_device(): lax.psum_scatter(jnp.dot(piece, w_output, preferred_element_type=jnp.floa...  142 us
    convert_element_type x4, other arithmetic, attend_back(): d_scores = (chance * (d_chance - jnp.sum(d_chance * chance, axis=-1, keep...  114 us
    all_gather x1, waiting for transfers between devices, per_device(): back_full = lax.all_gather(grad_out, 'mp', axis=0, tiled=True)  103 us
  transfers between devices with their start and end apart: 15, of which 10 were waited for; matrix products, arithmetic and copies ran while one was open for 34% of the time, Pallas kernels for 0%

commit v1 on v0

v1 whole, which is shorter than its diff:
```python
import functools
import math

import jax
import jax.numpy as jnp
from jax import lax
from jax.experimental import pallas as pl
from jax.experimental.pallas import tpu as pltpu
from jax.sharding import PartitionSpec as P

HD = 64
LANES = 128
UNIT = 1024
BF = jnp.bfloat16
F32 = jnp.float32

norm_eps = 1e-05
score_scale = 0.125

NT = (((1,), (1,)), ((), ()))
TN = (((0,), (0,)), ((), ()))
NN = (((1,), (0,)), ((), ()))
VMEM_LIMIT = 60 * 1024 * 1024


def mm(a, b, dims=NN):
    return lax.dot_general(a, b, dims, preferred_element_type=F32)


def call(body, *, flops, nbytes, trans=0, **kw):
    return pl.pallas_call(
        body,
        compiler_params=pltpu.CompilerParams(vmem_limit_bytes=VMEM_LIMIT),
        cost_estimate=pl.CostEstimate(flops=flops, bytes_accessed=nbytes, transcendentals=trans),
        **kw,
    )


def rope_table(places):
    half_dim = HD // 2
    freq_index = jnp.arange(half_dim, dtype=jnp.float32)
    base_freq = jnp.power(jnp.float32(500000.0), -2.0 * freq_index / HD)
    wave_len = 2.0 * math.pi / base_freq
    smooth = (8192.0 / wave_len - 1.0) / 3.0
    blended = (1.0 - smooth) * base_freq / 32.0 + smooth * base_freq
    frequency = jnp.where(
        wave_len < 2048.0, base_freq, jnp.where(wave_len > 8192.0, base_freq / 32.0, blended)
    )
    angles = places[:, None] * jnp.tile(frequency, LANES // half_dim)[None, :]
    return jnp.cos(angles), jnp.sin(angles)


def turn(t, cos_t, sin_t):
    lane = lax.broadcasted_iota(jnp.int32, t.shape, 1)
    first = (lane % HD) < (HD // 2)
    rot = jnp.where(first, -pltpu.roll(t, LANES - HD // 2, 1), pltpu.roll(t, HD // 2, 1))
    return t * cos_t + rot * sin_t


def qkv_body(n1_ref, w_ref, cos_ref, sin_ref, q_ref, kv_ref, *, qc, kc):
    parts, _, rows, cols = w_ref.shape
    y = mm(n1_ref[...], w_ref[...].reshape(parts * rows, cols))
    cos_t, sin_t = cos_ref[...], sin_ref[...]
    for c in range(0, qc, LANES):
        q_ref[:, c : c + LANES] = (
            turn(y[:, c : c + LANES], cos_t, sin_t) * score_scale
        ).astype(BF)
    if kc >= LANES:
        for c in range(0, kc, LANES):
            kv_ref[:, c : c + LANES] = turn(
                y[:, qc + c : qc + c + LANES], cos_t, sin_t
            ).astype(BF)
        kv_ref[:, kc:] = y[:, qc + kc :].astype(BF)
    else:
        both = y[:, qc : qc + LANES]
        lane = lax.broadcasted_iota(jnp.int32, both.shape, 1)
        kv_ref[...] = jnp.where(lane < kc, turn(both, cos_t, sin_t), both).astype(BF)


def qkv_call(n1, wqkv, cos_t, sin_t, qc, kc):
    rows, width = n1.shape
    dps, n, wr, cols = wqkv.shape
    return call(
        functools.partial(qkv_body, qc=qc, kc=kc),
        flops=2 * rows * width * n * cols,
        nbytes=2 * width * n * cols + 4 * rows * width,
        grid=(n,),
        in_specs=[
            pl.BlockSpec((rows, width), lambda j: (0, 0)),
            pl.BlockSpec((dps, 1, wr, cols), lambda j: (0, j, 0, 0)),
            pl.BlockSpec((rows, LANES), lambda j: (0, 0)),
            pl.BlockSpec((rows, LANES), lambda j: (0, 0)),
        ],
        out_specs=[
            pl.BlockSpec((rows, qc), lambda j: (0, j)),
            pl.BlockSpec((rows, 2 * kc), lambda j: (0, j)),
        ],
        out_shape=[
            jax.ShapeDtypeStruct((rows, n * qc), BF),
            jax.ShapeDtypeStruct((rows, n * 2 * kc), BF),
        ],
        name="qkv",
    )(n1, wqkv, cos_t, sin_t)


def half_views(x, half):
    wide = x.astype(F32)
    lane = lax.broadcasted_iota(jnp.int32, wide.shape, 1)
    kept = jnp.where((lane // HD) == half, wide, 0.0)
    moved = pltpu.roll(kept, HD, 1)
    low = jnp.where(half == 0, kept, moved)
    high = jnp.where(half == 0, moved, kept)
    return low.astype(BF), high.astype(BF)


def placed_views(x, half):
    wide = x.astype(F32)
    lane = lax.broadcasted_iota(jnp.int32, wide.shape, 1)
    swapped = pltpu.roll(wide, HD, 1)
    keep = (lane // HD) == half
    first = jnp.where(keep, jnp.where(half == 0, wide, swapped), 0.0)
    second = jnp.where(keep, jnp.where(half == 0, swapped, wide), 0.0)
    return first.astype(BF), second.astype(BF)


def fwd_body(info_ref, q_ref, *refs, n, tiles_per_kv):
    kv_refs = refs[:n]
    o_ref, lse_ref, m_sc, l_sc, acc_sc = refs[n:]
    i = pl.program_id(0)
    half = (i // tiles_per_kv) % 2
    count = info_ref[0]
    q = q_ref[...]
    rows = q.shape[0]
    upper = lax.broadcasted_iota(jnp.int32, (LANES, rows), 0) < HD

    def part(s):
        kv = kv_refs[s]
        ks = half_views(kv[:, :LANES], half)
        vs = half_views(kv[:, LANES:], half)
        added = None
        factors = []
        for h in range(2):
            scores = mm(ks[h], q, NT)
            if s == 0:
                key_at = lax.broadcasted_iota(jnp.int32, scores.shape, 0)
                row_at = lax.broadcasted_iota(jnp.int32, scores.shape, 1)
                scores = jnp.where(key_at <= row_at, scores, -1e30)
            top = jnp.max(scores, axis=0, keepdims=True)
            if s > 0:
                old = m_sc[h : h + 1, :]
                top = jnp.maximum(top, old)
            raised = jnp.exp(scores - top)
            total = jnp.sum(raised, axis=0, keepdims=True)
            if s > 0:
                factor = jnp.exp(old - top)
                factors.append(factor)
                total = total + l_sc[h : h + 1, :] * factor
            m_sc[h : h + 1, :] = top
            l_sc[h : h + 1, :] = total
            piece = mm(vs[h], raised.astype(BF), TN)
            added = piece if added is None else added + piece
        if s > 0:
            added = added + acc_sc[...] * jnp.where(upper, factors[0], factors[1])
        acc_sc[...] = added

    part(0)
    for s in range(1, n):
        pl.when(s <= count)(functools.partial(part, s))
    sums = l_sc[...]
    done = acc_sc[...] / jnp.where(upper, sums[0:1, :], sums[1:2, :])
    o_ref[...] = done.T.astype(BF)
    lse_ref[0] = m_sc[...] + jnp.log(sums)


def fwd_call(info, q, kvs):
    rows, width = q.shape
    n = len(kvs)
    tiles = width // LANES
    pairs = kvs[0].shape[1] // (2 * LANES)
    per_pair = tiles // pairs
    return call(
        functools.partial(fwd_body, n=n, tiles_per_kv=per_pair // 2),
        flops=4 * rows * rows * n * width,
        nbytes=4 * rows * width + 2 * n * rows * kvs[0].shape[1],
        trans=rows * rows * n * width // HD,
        grid_spec=pltpu.PrefetchScalarGridSpec(
            num_scalar_prefetch=1,
            grid=(tiles,),
            in_specs=[pl.BlockSpec((rows, LANES), lambda i, _: (0, i))]
            + [pl.BlockSpec((rows, 2 * LANES), lambda i, _: (0, i // per_pair))] * n,
            out_specs=[
                pl.BlockSpec((rows, LANES), lambda i, _: (0, i)),
                pl.BlockSpec((1, 8, rows), lambda i, _: (i, 0, 0)),
            ],
            scratch_shapes=[
                pltpu.VMEM((8, rows), F32),
                pltpu.VMEM((8, rows), F32),
                pltpu.VMEM((LANES, rows), F32),
            ],
        ),
        out_shape=[
            jax.ShapeDtypeStruct((rows, width), BF),
            jax.ShapeDtypeStruct((tiles, 8, rows), F32),
        ],
        name="attend",
    )(info, q, *kvs)


def bwd_body(info_ref, q_ref, do_ref, o_ref, lse_ref, *refs, dists, per_pair, first, last):
    refs = list(refs)
    kv_refs = [refs.pop(0) for _ in dists]
    before_ref = None if first else refs.pop(0)
    cos_ref, sin_ref = (refs.pop(0), refs.pop(0)) if last else (None, None)
    dq_ref = refs.pop(0)
    dkv_refs = [refs.pop(0) for _ in dists]
    dq_sc, dkv_sc = refs
    i = pl.program_id(0)
    place = i % per_pair
    half = place // (per_pair // 2)
    count = info_ref[0]
    q = q_ref[...]
    do = do_ref[...]
    rows = q.shape[0]

    @pl.when(place == 0)
    def _():
        dkv_sc[...] = jnp.zeros_like(dkv_sc)

    dq_sc[...] = jnp.zeros_like(dq_sc) if first else before_ref[0]
    prod = (do.astype(F32) * o_ref[...].astype(F32)).T
    deltas = [
        jnp.sum(prod[h * HD : (h + 1) * HD], axis=0, keepdims=True) for h in range(2)
    ]
    qs = placed_views(q, half)
    ds_ = placed_views(do, half)

    def part(at, s):
        kv = kv_refs[at]
        ks = half_views(kv[:, :LANES], half)
        vs = half_views(kv[:, LANES:], half)
        for h in range(2):
            scores = mm(ks[h], q, NT)
            chance = jnp.exp(scores - lse_ref[0, h : h + 1, :])
            if s == 0:
                key_at = lax.broadcasted_iota(jnp.int32, scores.shape, 0)
                row_at = lax.broadcasted_iota(jnp.int32, scores.shape, 1)
                chance = jnp.where(key_at <= row_at, chance, 0.0)
            d_chance = mm(vs[h], do, NT)
            d_scores = (chance * (d_chance - deltas[h])).astype(BF)
            dkv_sc[at, :, :LANES] += mm(d_scores, qs[h])
            dkv_sc[at, :, LANES:] += mm(chance.astype(BF), ds_[h])
            dq_sc[...] += mm(ks[h], d_scores, TN)

    for at, s in enumerate(dists):
        if s == 0:
            part(at, s)
        else:
            pl.when(s <= count)(functools.partial(part, at, s))

    if last:
        dq = dq_sc[...].T * score_scale
        dq_ref[...] = turn(dq, cos_ref[...], -sin_ref[...]).astype(BF)
    else:
        dq_ref[0] = dq_sc[...]

    @pl.when(place == per_pair - 1)
    def _():
        for at in range(len(dists)):
            dkv_refs[at][...] = dkv_sc[at].astype(BF)


def bwd_call(info, q, do, o, lse, kvs, dists, before, tables):
    rows, width = q.shape
    tiles = width // LANES
    wide = kvs[0].shape[1]
    per_pair = tiles // (wide // (2 * LANES))
    first, last = before is None, tables is not None
    col = pl.BlockSpec((rows, LANES), lambda i, _: (0, i))
    pair = pl.BlockSpec((rows, 2 * LANES), lambda i, _: (0, i // per_pair))
    turned = pl.BlockSpec((1, LANES, rows), lambda i, _: (i, 0, 0))
    fixed = pl.BlockSpec((rows, LANES), lambda i, _: (0, 0))
    m = len(dists)
    extra = [] if first else [before]
    extra += list(tables) if last else []
    return call(
        functools.partial(bwd_body, dists=dists, per_pair=per_pair, first=first, last=last),
        flops=10 * rows * rows * m * width,
        nbytes=10 * rows * width + 4 * m * rows * wide,
        trans=rows * rows * m * width // HD,
        grid_spec=pltpu.PrefetchScalarGridSpec(
            num_scalar_prefetch=1,
            grid=(tiles,),
            in_specs=[col, col, col, pl.BlockSpec((1, 8, rows), lambda i, _: (i, 0, 0))]
            + [pair] * m
            + ([] if first else [turned])
            + ([fixed, fixed] if last else []),
            out_specs=[col if last else turned] + [pair] * m,
            scratch_shapes=[
                pltpu.VMEM((LANES, rows), F32),
                pltpu.VMEM((m, rows, 2 * LANES), F32),
            ],
        ),
        out_shape=[
            jax.ShapeDtypeStruct((rows, width), BF)
            if last
            else jax.ShapeDtypeStruct((tiles, LANES, rows), F32)
        ]
        + [jax.ShapeDtypeStruct((rows, wide), BF)] * m,
        name="attend_back",
    )(info, q, do, o, lse, *[kvs[s] for s in dists], *extra)


def unturn_body(a_ref, b_ref, cos_ref, sin_ref, o_ref):
    t = a_ref[...].astype(F32) + b_ref[...].astype(F32)
    o_ref[:, :LANES] = turn(t[:, :LANES], cos_ref[...], -sin_ref[...]).astype(BF)
    o_ref[:, LANES:] = t[:, LANES:].astype(BF)


def unturn_call(a, b, cos_t, sin_t):
    rows, wide = a.shape
    blk = pl.BlockSpec((rows, 2 * LANES), lambda i: (0, i))
    fixed = pl.BlockSpec((rows, LANES), lambda i: (0, 0))
    return call(
        unturn_body,
        flops=8 * rows * wide,
        nbytes=6 * rows * wide,
        grid=(wide // (2 * LANES),),
        in_specs=[blk, blk, fixed, fixed],
        out_specs=blk,
        out_shape=jax.ShapeDtypeStruct((rows, wide), BF),
        name="unturn",
    )(a, b, cos_t, sin_t)


def out_body(o_ref, w_ref, x_ref, gain_ref, mid_ref, n2_ref, acc):
    j = pl.program_id(0)
    _, n, wr, cols = w_ref.shape
    acc[j] = mm(o_ref[...], w_ref[...].reshape(n * wr, cols))

    @pl.when(j == pl.num_programs(0) - 1)
    def _():
        parts = acc.shape[0]
        total = None
        for p in range(parts):
            at = slice(p * cols, (p + 1) * cols)
            mid = x_ref[:, at].astype(F32) + acc[p]
            mid_ref[:, at] = mid
            piece = jnp.sum(mid * mid, axis=1, keepdims=True)
            total = piece if total is None else total + piece
        inv = lax.rsqrt(total / (parts * cols) + norm_eps)
        for p in range(parts):
            at = slice(p * cols, (p + 1) * cols)
            n2_ref[:, at] = (mid_ref[:, at] * inv * gain_ref[:, at]).astype(BF)


def out_call(o, wo, x, gain):
    rows, width = x.shape
    dps, n, wr, cols = wo.shape
    full = pl.BlockSpec((rows, width), lambda j: (0, 0))
    return call(
        out_body,
        flops=2 * rows * width * n * wr,
        nbytes=2 * width * n * wr + 12 * rows * width,
        grid=(dps,),
        in_specs=[
            pl.BlockSpec((rows, n * wr), lambda j: (0, 0)),
            pl.BlockSpec((1, n, wr, cols), lambda j: (j, 0, 0, 0)),
            full,
            pl.BlockSpec((1, width), lambda j: (0, 0)),
        ],
        out_specs=[full, full],
        out_shape=[
            jax.ShapeDtypeStruct((rows, width), F32),
            jax.ShapeDtypeStruct((rows, width), BF),
        ],
        scratch_shapes=[pltpu.VMEM((dps, rows, cols), F32)],
        name="out_proj",
    )(o, wo, x, gain)


def ffn_body(n2_ref, g_ref, wg_ref, wu_ref, wd_ref, *refs, first):
    if not first:
        refs = refs[5:]
    n2_all, g_all, hid_all, dg_all, du_all, ffn_ref, dn_ref, ffn_acc, dn_acc = refs
    f = pl.program_id(0)
    n2 = n2_ref[...]
    g = g_ref[...]

    @pl.when(f == 0)
    def _():
        n2_all[...] = n2
        g_all[...] = g

    wg, wu, wd = wg_ref[...], wu_ref[...], wd_ref[...]
    gate = mm(n2, wg)
    up = mm(n2, wu)
    d_hid = mm(g, wd, NT)
    sig = jax.nn.sigmoid(gate)
    act = gate * sig
    hid = (act * up).astype(BF)
    d_gate = (d_hid * up * sig * (1.0 + gate * (1.0 - sig))).astype(BF)
    d_up = (d_hid * act).astype(BF)
    hid_all[...] = hid
    dg_all[...] = d_gate
    du_all[...] = d_up
    ffn = mm(hid, wd)
    dn = mm(d_gate, wg, NT) + mm(d_up, wu, NT)

    @pl.when(f == 0)
    def _():
        ffn_acc[...] = ffn
        dn_acc[...] = dn

    @pl.when(f > 0)
    def _():
        ffn_acc[...] += ffn
        dn_acc[...] += dn

    @pl.when(f == pl.num_programs(0) - 1)
    def _():
        ffn_ref[...] = ffn_acc[...].astype(BF)
        dn_ref[...] = dn_acc[...].astype(BF)


def ffn_call(n2, g, wg, wu, wd, s, n, big):
    rows, width = n2.shape
    ff = wg.shape[1]
    tf = min(512, ff)
    first = big is None
    full = pl.BlockSpec((rows, width), lambda f: (0, 0))
    wcol = pl.BlockSpec((width, tf), lambda f: (0, f))
    wide_all = pl.BlockSpec((rows, width), lambda f: (s, 0))
    tile_all = pl.BlockSpec((rows, tf), lambda f: (s, f))
    any_spec = pl.BlockSpec(memory_space=pl.ANY)
    out = call(
        functools.partial(ffn_body, first=first),
        flops=12 * rows * width * ff,
        nbytes=6 * width * ff + 12 * rows * width + 6 * rows * ff,
        grid=(ff // tf,),
        in_specs=[full, full, wcol, wcol, pl.BlockSpec((tf, width), lambda f: (f, 0))]
        + ([] if first else [any_spec] * 5),
        out_specs=[wide_all, wide_all, tile_all, tile_all, tile_all, full, full],
        out_shape=[jax.ShapeDtypeStruct((n * rows, width), BF)] * 2
        + [jax.ShapeDtypeStruct((n * rows, ff), BF)] * 3
        + [jax.ShapeDtypeStruct((rows, width), BF)] * 2,
        scratch_shapes=[pltpu.VMEM((rows, width), F32), pltpu.VMEM((rows, width), F32)],
        input_output_aliases={} if first else {5 + k: k for k in range(5)},
        name="ffn",
    )(n2, g, wg, wu, wd, *([] if first else big))
    return out[:5], out[5], out[6]


def do_body(da_ref, w_ref, do_ref):
    dps, _, wr, cols = w_ref.shape
    total = None
    for p in range(dps):
        piece = mm(da_ref[:, p * cols : (p + 1) * cols], w_ref[p, 0], NT)
        total = piece if total is None else total + piece
    do_ref[...] = total.astype(BF)


def do_call(da, wo):
    rows, width = da.shape
    dps, n, wr, cols = wo.shape
    return call(
        do_body,
        flops=2 * rows * width * n * wr,
        nbytes=2 * width * n * wr + 4 * rows * width,
        grid=(n,),
        in_specs=[
            pl.BlockSpec((rows, width), lambda j: (0, 0)),
            pl.BlockSpec((dps, 1, wr, cols), lambda j: (0, j, 0, 0)),
        ],
        out_specs=pl.BlockSpec((rows, wr), lambda j: (0, j)),
        out_shape=jax.ShapeDtypeStruct((rows, n * wr), BF),
        name="d_o",
    )(da, wo)


def dn1_body(dq_ref, dkv_ref, w_ref, out_ref, *, qc):
    _, n, wr, cols = w_ref.shape
    kc2 = cols - qc
    total = None
    for j in range(n):
        w = w_ref[0, j]
        piece = mm(dq_ref[:, j * qc : (j + 1) * qc], w[:, :qc], NT) + mm(
            dkv_ref[:, j * kc2 : (j + 1) * kc2], w[:, qc:], NT
        )
        total = piece if total is None else total + piece
    out_ref[...] = total


def dn1_call(dq, dkv, wqkv, qc):
    rows = dq.shape[0]
    dps, n, wr, cols = wqkv.shape
    return call(
        functools.partial(dn1_body, qc=qc),
        flops=2 * rows * dps * wr * n * cols,
        nbytes=2 * dps * wr * n * cols + 4 * rows * dps * wr,
        grid=(dps,),
        in_specs=[
            pl.BlockSpec(dq.shape, lambda p: (0, 0)),
            pl.BlockSpec(dkv.shape, lambda p: (0, 0)),
            pl.BlockSpec((1, n, wr, cols), lambda p: (p, 0, 0, 0)),
        ],
        out_specs=pl.BlockSpec((rows, wr), lambda p: (0, p)),
        out_shape=jax.ShapeDtypeStruct((rows, dps * wr), F32),
        name="d_n1",
    )(dq, dkv, wqkv)


def dw_body(blk_ref, l0_ref, l1_ref, r_ref, *refs, add):
    add_ref = refs[0] if add else None
    out_ref, left = refs[-2:]
    wr = l0_ref.shape[1]

    @pl.when(pl.program_id(1) == 0)
    def _():
        left[:wr] = l0_ref[...].T
        left[wr:] = l1_ref[...].T

    y = mm(left[...], r_ref[...])
    for k in range(2):
        part = y[k * wr : (k + 1) * wr]
        if add:
            part = part + add_ref[k].astype(F32)
        out_ref[k] = part.astype(BF)


def dw_call(blocks, lhs, rhs, wr, extra):
    half = blocks.shape[0]
    toks, cols = lhs.shape[0], rhs.shape[1]
    tn = min(cols, 512 if toks > 1024 else 1024)
    out = pl.BlockSpec((2, wr, tn), lambda t, c, _: (t, 0, c))
    return call(
        functools.partial(dw_body, add=extra is not None),
        flops=2 * toks * cols * half * wr,
        nbytes=2 * (toks * cols + half * wr * (toks + 2 * cols)),
        grid_spec=pltpu.PrefetchScalarGridSpec(
            num_scalar_prefetch=1,
            grid=(half // 2, cols // tn),
            in_specs=[
                pl.BlockSpec((toks, wr), lambda t, c, blk: (0, blk[2 * t])),
                pl.BlockSpec((toks, wr), lambda t, c, blk: (0, blk[2 * t + 1])),
                pl.BlockSpec((toks, tn), lambda t, c, _: (0, c)),
            ]
            + ([] if extra is None else [out]),
            out_specs=out,
            scratch_shapes=[pltpu.VMEM((2 * wr, toks), BF)],
        ),
        out_shape=jax.ShapeDtypeStruct((half, wr, cols), BF),
        name="dw",
    )(blocks, lhs, lhs, rhs, *([] if extra is None else [extra]))


def norm_back(values, inv_root, gain_vec, d_norm):
    scaled = d_norm * gain_vec
    inner_sum = jnp.mean(scaled * values, axis=-1, keepdims=True)
    d_values = inv_root * scaled - values * (inv_root * inv_root * inv_root) * inner_sum
    return (d_values, jnp.sum(d_norm * values * inv_root, axis=0))


def plus(a, b):
    return (a.astype(F32) + b.astype(F32)).astype(BF)


def advance(main, tasks):
    held = [task[1] for task in tasks]
    main, held = lax.optimization_barrier((main, held))
    for task, values in zip(tasks, held):
        if task[1]:
            try:
                task[1] = task[0].send(values)
            except StopIteration as end:
                task[1], task[2] = [], end.value
    return main


def task_of(steps):
    return [steps, next(steps), None]


def finish(task):
    while task[1]:
        try:
            task[1] = task[0].send(task[1])
        except StopIteration as end:
            task[1], task[2] = [], end.value
    return task[2]


def spread_sum(x, name, size):
    step = 1
    while step < size:
        x = x + lax.ppermute(x, name, [(i, i ^ step) for i in range(size)])
        step *= 2
    return x


def per_device(
    tokens,
    segment_ids,
    grad_out,
    attn_gain,
    w_query,
    w_key,
    w_value,
    w_output,
    ffn_gain,
    w_gate,
    w_up,
    w_down,
    *,
    dps,
    n,
):
    rows, width = tokens.shape
    qc, kc = w_query.shape[1], w_key.shape[1]
    zi = lax.axis_index("mp")
    di = lax.axis_index("dp")
    ring = [(i, (i + 1) % n) for i in range(n)]
    up_chain = [(i, i + 1) for i in range(n - 1)]
    down_chain = [(i + 1, i) for i in range(n - 1)]
    x = tokens.astype(F32)
    gain_one = attn_gain.astype(F32)
    gain_two = ffn_gain.astype(F32)

    wr = width // dps
    piece = jnp.concatenate(
        [lax.dynamic_slice_in_dim(w, di * wr, wr, 0) for w in (w_query, w_key, w_value)], axis=1
    )
    wqkv = lax.all_gather(piece, ("dp", "mp"), axis=0).reshape(dps, n, wr, qc + 2 * kc)
    oc = width // dps
    wo_piece = lax.dynamic_slice_in_dim(w_output, di * oc, oc, 1)
    wo = lax.all_gather(wo_piece, ("dp", "mp"), axis=0).reshape(dps, n, w_output.shape[0], oc)

    row_index = zi * rows + jnp.arange(rows, dtype=jnp.int32)
    own_seg = lax.dynamic_slice_in_dim(segment_ids, zi * rows, rows, 0)
    first_row = jnp.sum((segment_ids[None, :] < own_seg[:, None]).astype(jnp.int32), axis=1)
    cos_t, sin_t = rope_table((row_index - first_row).astype(F32))
    count = zi - first_row[0] // rows
    info = jnp.reshape(count, (1,)).astype(jnp.int32)

    inv_one = lax.rsqrt(jnp.mean(x * x, axis=-1, keepdims=True) + norm_eps)
    n1 = (x * inv_one * gain_one).astype(BF)

    gs = [grad_out]
    for s in range(1, n - 1):
        gs.append(lax.ppermute(gs[-1], "mp", ring))
    n1, *gs = lax.optimization_barrier((n1, *gs))
    q, kv = qkv_call(n1, wqkv, cos_t, sin_t, qc, kc)
    if kc < LANES:
        fold = LANES // kc
        kv = (
            kv.reshape(rows, n // fold, fold, 2, kc)
            .transpose(0, 1, 3, 2, 4)
            .reshape(rows, n * 2 * kc)
        )
    kvs = [kv]
    for s in range(1, n):
        kvs.append(lax.ppermute(kvs[-1], "mp", up_chain))
    late, kvs[-1] = lax.optimization_barrier((gs[-1], kvs[-1]))
    gs.append(lax.ppermute(late, "mp", ring))

    o, lse = fwd_call(info, q, kvs)
    mid, n2 = out_call(o, wo, tokens, gain_two.reshape(1, width))

    n2s = [n2]
    for s in range(1, n):
        n2s.append(lax.ppermute(n2s[-1], "mp", ring))
    big, t, own_dn = None, None, None
    ffn_parts = []
    for s in range(n):
        n2c = n2s[s]
        if s >= 3:
            n2c, t = lax.optimization_barrier((n2c, t))
        big, part, dn = ffn_call(n2c, gs[s], w_gate, w_up, w_down, s, n, big)
        ffn_parts.append(part)
        if s == 0:
            own_dn = dn
        elif s == 1:
            t = dn
        elif s < n - 1:
            t = plus(lax.ppermute(t, "mp", ring), dn)
    n2_all, g_all, hid_all, dg_all, du_all = big

    core = di % 2
    pairs = jnp.arange(dps // 2, dtype=jnp.int32) * 2
    fixed_ids = [pairs + (core ^ c) for c in range(2)]
    swap = [(i, i ^ 1) for i in range(dps)]
    jobs = ((n2_all, dg_all), (n2_all, du_all), (g_all, hid_all))
    got = lax.ppermute(t, "mp", ring)
    away = [dw_call(fixed_ids[1], a, b, wr, None) for a, b in jobs]
    got, away = lax.optimization_barrier((got, away))
    got = lax.ppermute(plus(got, dn), "mp", ring)
    away = [lax.ppermute(a, "dp", swap) for a in away]
    kept = [dw_call(fixed_ids[0], a, b, wr, e) for (a, b), e in zip(jobs, away)]
    got, kept = lax.optimization_barrier((got, kept))
    d_n2 = got.astype(F32) + own_dn.astype(F32)
    d_n2, ffn_parts = lax.optimization_barrier((d_n2, ffn_parts))

    def ffn_ring():
        t = ffn_parts[1]
        for s in range(2, n):
            t = plus(lax.ppermute(t, "mp", ring), ffn_parts[s])
            (t,) = yield [t]
        t = lax.ppermute(t, "mp", ring)
        return (mid + t.astype(F32) + ffn_parts[0].astype(F32)).astype(BF)

    inv_two = lax.rsqrt(jnp.mean(mid * mid, axis=-1, keepdims=True) + norm_eps)
    d_from_two, gain_two_part = norm_back(mid, inv_two, gain_two, d_n2)
    d_mid = grad_out.astype(F32) + d_from_two
    da = d_mid.astype(BF)
    do = do_call(da, wo)

    moving_ids = [di ^ (pairs + c) for c in range(2)]

    def cube(lhs, rhs):
        away = lax.ppermute(dw_call(moving_ids[1], lhs, rhs, wr, None), "dp", swap)
        near = dw_call(moving_ids[0], lhs, rhs, wr, away)
        (near,) = yield [near]
        bits = (dps // 2).bit_length() - 1
        wide = near.shape[2] // 2
        ts = [
            near[:, :, k * wide : (k + 1) * wide].reshape((2,) * bits + (wr, wide))
            for k in range(2)
        ]
        left = [list(range(bits)), list(range(bits))]
        for step in range(bits):
            for k in range(2):
                bit = left[k][-1 if k else 0]
                axis = left[k][::-1].index(bit)
                left[k].remove(bit)
                perm = [(i, i ^ (2 << bit)) for i in range(dps)]
                away = lax.ppermute(
                    lax.index_in_dim(ts[k], 1, axis, keepdims=False), "dp", perm
                )
                ts[k] = plus(lax.index_in_dim(ts[k], 0, axis, keepdims=False), away)
            ts = yield ts
        return jnp.concatenate(ts, axis=1).reshape(wr, n, -1)

    two_core = [[i for i in range(dps) if i % 2 == c] for c in range(2)]

    def over_dp(g):
        return lax.psum_scatter(
            g, "dp", scatter_dimension=0, axis_index_groups=two_core, tiled=False
        ).astype(F32)

    gate_sum, up_sum, down_sum = [over_dp(g) for g in kept]
    wo_task = task_of(cube(da, o))
    ffn_task = task_of(ffn_ring())
    before = None
    travel = None
    for at, s in enumerate(reversed(range(n))):
        tables = (cos_t, sin_t) if s == 0 else None
        before, dkv = bwd_call(info, q, do, o, lse, kvs, (s,), before, tables)
        if travel is not None and s > 0:
            dkv = plus(lax.ppermute(travel, "mp", down_chain), dkv)
        tasks = [wo_task] + ([ffn_task] if at % 2 else [])
        if s > 0:
            before, travel = advance((before, dkv), tasks)
        else:
            before, dkv = advance((before, dkv), tasks)
            dkv_own = unturn_call(lax.ppermute(travel, "mp", down_chain), dkv, cos_t, sin_t)
    dq = before
    wo_cube = finish(wo_task)
    if kc < LANES:
        dkv_own = (
            dkv_own.reshape(rows, n // fold, 2, fold, kc)
            .transpose(0, 1, 3, 2, 4)
            .reshape(rows, n * 2 * kc)
        )
    cubes = [finish(task_of(cube(n1, dq))), finish(task_of(cube(n1, dkv_own))), wo_cube]
    w_cube = jnp.concatenate(cubes, axis=2)
    d_n1 = dn1_call(dq, dkv_own, wqkv, qc)
    layer_out = finish(ffn_task)
    d_from_one, gain_one_part = norm_back(x, inv_one, gain_one, d_n1)
    grad_tokens = (d_mid + d_from_one).astype(BF)

    gains = jnp.stack([gain_one_part, gain_two_part])
    gains = spread_sum(spread_sum(gains, "mp", n), "dp", dps)

    def over_mp(g):
        return lax.psum_scatter(g, "mp", scatter_dimension=1, tiled=False).astype(F32)

    w_sum = over_mp(w_cube)
    cols = qc + 2 * kc
    return (
        layer_out,
        grad_tokens,
        gains[0],
        w_sum[:, :qc],
        w_sum[:, qc : qc + kc],
        w_sum[:, qc + kc : cols],
        w_sum[:, cols:].T,
        gains[1],
        gate_sum,
        up_sum,
        down_sum.T,
    )


def solution(mesh):
    rows = P(("dp", "mp"), None)
    col = P(None, "mp")
    row = P("mp", None)
    placed = (rows, P("dp"), rows, P(), col, col, col, row, P(), col, col, row)
    body = functools.partial(per_device, dps=mesh.shape["dp"], n=mesh.shape["mp"])
    return jax.shard_map(
        body,
        mesh=mesh,
        in_specs=placed,
        out_specs=(
            rows,
            rows,
            P(),
            P("dp", "mp"),
            P("dp", "mp"),
            P("dp", "mp"),
            P("mp", "dp"),
            P(),
            P("dp", "mp"),
            P("dp", "mp"),
            P("mp", "dp"),
        ),
        check_vma=False,
    )
```

time: 2280 us -> 1250 us (0.55)
  matrix products: 732 us -> 0 us
  waiting for transfers between devices: 1060 us -> 524 us
  Pallas kernels: 0 us -> 465 us
  other arithmetic: 254 us -> 79.6 us
  local copies, waits for them, and re-layouts: 164 us -> 29 us
  starting transfers between devices: 0.62 us -> 131 us
  blocking collectives: 46 us -> 0 us
    dot_general x49 -> x0, matrix products: 732 us -> none  [the longest x8 163 us: block_scores(): jnp.einsum('qgrd,kgd->grqk', query_block, key_rot, preferred_element_type...]
    reduce_scatter x11 -> x1, waiting for transfers between devices: 580 us -> 0.01 us  [over_mp(): lax.psum_scatter(g, 'mp', scatter_dimension=1, tiled=False).astype(F32)]
    ppermute x0 -> x41, waiting for transfers between devices: none -> 506 us  [the longest x2 131 us: per_device(): gs.append(lax.ppermute(gs[-1], 'mp', ring))]
    pallas_call x0 -> x26, Pallas kernels: none -> 465 us  [the longest x4 166 us: ffn_call(): call(functools.partial(ffn_body, first=first), flops=12 * rows * width *...]
    all_gather x4 -> x2, waiting for transfers between devices: 477 us -> 18.5 us  [the longest x1 18.5 us: per_device(): lax.all_gather(piece, ('dp', 'mp'), axis=0).reshape(dps, n, wr, qc + 2 * kc)]
    ppermute x0 -> x41, starting transfers between devices: none -> 130 us  [the longest x12 37.5 us: cube(): lax.ppermute(lax.index_in_dim(ts[k], 1, axis, keepdims=False), 'dp', perm)]
    dynamic_update_slice x20 -> x0, local copies, waits for them, and re-layouts: 103 us -> none  [the longest x8 92.6 us: per_device(): lax.scan(attend_back, (zero_heads, zero_heads), (query_blocks, seg_blocks...]
    convert_element_type x24 -> x28, other arithmetic: 156 us -> 55.3 us  [the longest x18 31.8 us: plus(): return (a.astype(F32) + b.astype(F32)).astype(BF)]
  transfers between devices with their start and end apart: 15 -> 47, of which waited for: 10 -> 24; matrix products, arithmetic and copies ran while one was open for 34% -> 8% of each run, Pallas kernels for 0% -> 36%
where the time goes in v1:
time: 1250 us
  waiting for transfers between devices  524 us (42%)
  Pallas kernels  465 us (37%)
  starting transfers between devices  131 us (10%)
  other arithmetic  79.6 us (6%)
  local copies, waits for them, and re-layouts  29 us (2%)
  between operations  17.5 us (1%)
    pallas_call x4, Pallas kernels, ffn_call(): call(functools.partial(ffn_body, first=first), flops=12 * rows * width *...  166 us
    pallas_call x12, Pallas kernels, dw_call(): call(functools.partial(dw_body, add=extra is not None), flops=2 * toks *...  150 us
    ppermute x2, waiting for transfers between devices, per_device(): gs.append(lax.ppermute(gs[-1], 'mp', ring))  131 us
    ppermute x3, waiting for transfers between devices, per_device(): kvs.append(lax.ppermute(kvs[-1], 'mp', up_chain))  97.1 us
    ppermute x3, waiting for transfers between devices, per_device(): n2s.append(lax.ppermute(n2s[-1], 'mp', ring))  88.1 us
    pallas_call x4, Pallas kernels, bwd_call(): call(functools.partial(bwd_body, dists=dists, per_pair=per_pair, first=fi...  76 us
    ppermute x1, waiting for transfers between devices, ffn_ring(): t = lax.ppermute(t, 'mp', ring)  63.8 us
    ppermute x12, waiting for transfers between devices, cube(): lax.ppermute(lax.index_in_dim(ts[k], 1, axis, keepdims=False), 'dp', perm)  58.4 us
  transfers between devices with their start and end apart: 47, of which 24 were waited for; matrix products, arithmetic and copies ran while one was open for 8% of the time, Pallas kernels for 36%

profile of v1, /device:TPU:0, one launch (start us, length us, event | category | flops | bytes accessed | tf_op | source)
XLA Modules:
  0.0 1246.3 jit_solution(1363085786170409965)
XLA Ops:
  12.5 3.1 collective-permute-start
  15.6 56.4 %collective-permute-done.g_ref = bf16[512,2048]{1,0:T(8,128)(2,1)} collective-permute-done((bf16[512,2048]{1,0:T(8,128)(2,1)}, bf16[512,2048]{1,0:T(8,128)(2,1)}, u32[]{:S(2)}, u32[]{:S(2)}) %collective-permute-start) | collective-permute-done | bytes 2097184 | tf_op jit(solution)/shard_map/ppermute | solution.py:649
  81.3 74.1 %collective-permute-done.1.g_ref = bf16[512,2048]{1,0:T(8,128)(2,1)} collective-permute-done((bf16[512,2048]{1,0:T(8,128)(2,1)}, bf16[512,2048]{1,0:T(8,128)(2,1)}, u32[]{:S(2)}, u32[]{:S(2)}) %collective-permute-start.1) | collective-permute-done | bytes 2097184 | tf_op jit(solution)/shard_map/ppermute | solution.py:649
  155.5 18.5 %all-gather.5.cloned.1.call-done = bf16[8192,768]{1,0:T(8,128)(2,1)} async-done(((bf16[256,768]{1,0:T(8,128)(2,1)}), bf16[8192,768]{1,0:T(8,128)(2,1)}) %all-gather.5.cloned.1.call-update) | async-done | bytes 12582928 | tf_op jit(solution)/shard_map/all_gather | solution.py:632
  174.0 12.1 qkv.1
  187.5 38.1 %collective-permute-done.2.refs_1_.refs_0_ = bf16[512,1024]{1,0:T(8,128)(2,1)S(1)} collective-permute-done((bf16[512,1024]{1,0:T(8,128)(2,1)}, bf16[512,1024]{1,0:T(8,128)(2,1)S(1)}, u32[]{:S(2)}, u32[]{:S(2)}) %collective-permute-start.2) | collective-permute-done | bytes 1048608 | tf_op jit(solution)/shard_map/ppermute | solution.py:661
  225.6 4.3 collective-permute-start.3
  229.9 43.3 %collective-permute-done.3.refs_2_.refs_0_ = bf16[512,1024]{1,0:T(8,128)(2,1)S(1)} collective-permute-done((bf16[512,1024]{1,0:T(8,128)(2,1)S(1)}, bf16[512,1024]{1,0:T(8,128)(2,1)S(1)}, u32[]{:S(2)}, u32[]{:S(2)}) %collective-permute-start.3) | collective-permute-done | bytes 1048608 | tf_op jit(solution)/shard_map/ppermute | solution.py:661
  273.2 5.9 collective-permute-start.4
  283.4 15.8 %collective-permute-done.4.refs_3_.refs_0_ = bf16[512,1024]{1,0:T(8,128)(2,1)} collective-permute-done((bf16[512,1024]{1,0:T(8,128)(2,1)S(1)}, bf16[512,1024]{1,0:T(8,128)(2,1)}, u32[]{:S(2)}, u32[]{:S(2)}) %collective-permute-start.4) | collective-permute-done | bytes 1048608 | tf_op jit(solution)/shard_map/ppermute | solution.py:661
  299.1 20.2 %attend.1 = (bf16[512,2048]{1,0:T(8,128)(2,1)}, f32[16,8,512]{2,1,0:T(8,128)}) custom-call(s32[1]{0:T(128)} %bitcast.1.info_ref, bf16[512,2048]{1,0:T(8,128)(2,1)} %get-tuple-element.90.q_ref, bf16[512,1024]{1,0:T(8,128)(2,1)} %get-tuple-element.91.refs_0_, bf16[512,1024]{1,0:T(8,128)(2,1)} %copy-done.26, bf16[512,1024]{1,0:T(8,128)(2,1)} %copy-done.27, ...), custom_call_target="tpu_custom_call" | custom-call | flops 8589934592 | bytes 8388608 | tf_op jit(solution)/shard_map/attend/pallas_call | solution.py:181
  319.4 13.8 %out_proj.1 = (f32[512,2048]{1,0:T(8,128)}, bf16[512,2048]{1,0:T(8,128)(2,1)}) custom-call(bf16[512,2048]{1,0:T(8,128)(2,1)} %get-tuple-element.94.o_ref.r_ref, bf16[8,4,512,256]{3,2,1,0:T(8,128)(2,1)} %bitcast.123, bf16[512,2048]{1,0:T(8,128)(2,1)} %x_ref.1, f32[1,2048]{1,0:T(1,128)} %bitcast.118), custom_call_target="tpu_custom_call" | custom-call | flops 4294967296 | bytes 20971520 | tf_op jit(solution)/shard_map/out_proj/pallas_call | solution.py:360
  333.2 20.5 %collective-permute-start.5 = (bf16[512,2048]{1,0:T(8,128)(2,1)}, bf16[512,2048]{1,0:T(8,128)(2,1)}, u32[]{:S(2)}, u32[]{:S(2)}) collective-permute-start(bf16[512,2048]{1,0:T(8,128)(2,1)} %get-tuple-element.96.n2_ref), channel_id=1, source_target_pairs={{0,1},{1,2},{2,3},{3,0},{4,5},{5,6},{6,7},{7,4},{8,9},{9,10},{10,1... | collective-permute-start | bytes 6291464 | tf_op jit(solution)/shard_map/ppermute | solution.py:670
  353.9 41.6 %ffn.4 = (bf16[2048,2048]{1,0:T(8,128)(2,1)}, bf16[2048,2048]{1,0:T(8,128)(2,1)}, bf16[2048,2048]{1,0:T(8,128)(2,1)}, bf16[2048,2048]{1,0:T(8,128)(2,1)}, bf16[2...) custom-call(bf16[512,2048]{1,0:T(8,128)(2,1)} %get-tuple-element.96.n2_ref, ...), custom_call_target="tpu_custom_call" | custom-call | flops 25769803776 | bytes 44040192 | tf_op jit(solution)/shard_map/ffn/pallas_call | solution.py:435
  395.4 4.6 collective-permute-done.5.n2_ref
  402.7 41.7 %ffn.5 = (bf16[2048,2048]{1,0:T(8,128)(2,1)}, bf16[2048,2048]{1,0:T(8,128)(2,1)}, bf16[2048,2048]{1,0:T(8,128)(2,1)}, bf16[2048,2048]{1,0:T(8,128)(2,1)}, bf16[2...) custom-call(bf16[512,2048]{1,0:T(8,128)(2,1)} %collective-permute-do, ...), custom_call_target="tpu_custom_call", output_to_operand_aliasing={{0}: (5, {}), {1}: (6, {}), {2}: (7, {}), {3}: (8, {}), {4}... | custom-call | flops 25769803776 | bytes 44040192 | tf_op jit(solution)/shard_map/ffn/pallas_call | solution.py:435
  444.5 45.4 %collective-permute-done.6.n2_ref = bf16[512,2048]{1,0:T(8,128)(2,1)} collective-permute-done((bf16[512,2048]{1,0:T(8,128)(2,1)}, bf16[512,2048]{1,0:T(8,128)(2,1)}, u32[]{:S(2)}, u32[]{:S(2)}) %collective-permute-start.6) | collective-permute-done | bytes 2097184 | tf_op jit(solution)/shard_map/ppermute | solution.py:670
  492.8 41.6 %ffn.6 = (bf16[2048,2048]{1,0:T(8,128)(2,1)}, bf16[2048,2048]{1,0:T(8,128)(2,1)}, bf16[2048,2048]{1,0:T(8,128)(2,1)}, bf16[2048,2048]{1,0:T(8,128)(2,1)}, bf16[2...) custom-call(bf16[512,2048]{1,0:T(8,128)(2,1)} %collective-permute-do, ...), custom_call_target="tpu_custom_call", output_to_operand_aliasing={{0}: (5, {}), {1}: (6, {}), {2}: (7, {}), {3}: (8, {}), {4}... | custom-call | flops 25769803776 | bytes 44040192 | tf_op jit(solution)/shard_map/ffn/pallas_call | solution.py:435
  534.8 3.8 add_convert_fusion.4
  538.6 38.1 %collective-permute-done.7.n2_ref = bf16[512,2048]{1,0:T(8,128)(2,1)} collective-permute-done((bf16[512,2048]{1,0:T(8,128)(2,1)}, bf16[512,2048]{1,0:T(8,128)(2,1)}, u32[]{:S(2)}, u32[]{:S(2)}) %collective-permute-start.7) | collective-permute-done | bytes 2097184 | tf_op jit(solution)/shard_map/ppermute | solution.py:670
  579.4 41.4 %ffn.7 = (bf16[2048,2048]{1,0:T(8,128)(2,1)}, bf16[2048,2048]{1,0:T(8,128)(2,1)}, bf16[2048,2048]{1,0:T(8,128)(2,1)}, bf16[2048,2048]{1,0:T(8,128)(2,1)}, bf16[2...) custom-call(bf16[512,2048]{1,0:T(8,128)(2,1)} %collective-permute-do, ...), custom_call_target="tpu_custom_call", output_to_operand_aliasing={{0}: (5, {}), {1}: (6, {}), {2}: (7, {}), {3}: (8, {}), {4}... | custom-call | flops 25769803776 | bytes 44040192 | tf_op jit(solution)/shard_map/ffn/pallas_call | solution.py:435
  620.8 17.7 %dw.13 = bf16[4,256,2048]{2,1,0:T(8,128)(2,1)} custom-call(s32[4]{0:T(128)} %fusion.21.blk_ref, bf16[2048,2048]{1,0:T(8,128)(2,1)} %get-tuple-element.119.l0_ref.l1_ref, bf16[2048,2048]{1,0:T(8,128)(2,1)} %get-tuple-element.119.l0_ref.l1_ref, bf16[2048,2048]{1,0:T(8,128)(2,1)} %get-tuple-element.121.r_ref), custom_call_target="tpu_custom_call" | custom-call | flops 8589934592 | bytes 20971520 | tf_op jit(solution)/shard_map/dw/pallas_call | solution.py:535
  638.6 17.7 %dw.12 = bf16[4,256,2048]{2,1,0:T(8,128)(2,1)} custom-call(s32[4]{0:T(128)} %fusion.21.blk_ref, bf16[2048,2048]{1,0:T(8,128)(2,1)} %get-tuple-element.119.l0_ref.l1_ref, bf16[2048,2048]{1,0:T(8,128)(2,1)} %get-tuple-element.119.l0_ref.l1_ref, bf16[2048,2048]{1,0:T(8,128)(2,1)} %get-tuple-element.120.r_ref), custom_call_target="tpu_custom_call" | custom-call | flops 8589934592 | bytes 20971520 | tf_op jit(solution)/shard_map/dw/pallas_call | solution.py:535
  656.3 17.7 %dw.14 = bf16[4,256,2048]{2,1,0:T(8,128)(2,1)} custom-call(s32[4]{0:T(128)} %fusion.21.blk_ref, bf16[2048,2048]{1,0:T(8,128)(2,1)} %get-tuple-element.122.l0_ref.l1_ref, bf16[2048,2048]{1,0:T(8,128)(2,1)} %get-tuple-element.122.l0_ref.l1_ref, bf16[2048,2048]{1,0:T(8,128)(2,1)} %get-tuple-element.123.r_ref), custom_call_target="tpu_custom_call" | custom-call | flops 8589934592 | bytes 20971520 | tf_op jit(solution)/shard_map/dw/pallas_call | solution.py:535
  677.7 3.8 add_convert_fusion.3
  681.5 17.5 %collective-permute-start.11 = (bf16[512,2048]{1,0:T(8,128)(2,1)}, bf16[512,2048]{1,0:T(8,128)(2,1)}, u32[]{:S(2)}, u32[]{:S(2)}) collective-permute-start(bf16[512,2048]{1,0:T(8,128)(2,1)} %add_convert_fusion.3), channel_id=1, source_target_pairs={{0,1},{1,2},{2,3},{3,0},{4,5},{5,6},{6,7},{7,4},{8,9},{9,10},{10,1... | collective-permute-start | bytes 6291464 | tf_op jit(solution)/shard_map/ppermute | solution.py:695
  699.0 18.1 %dw.17 = bf16[4,256,2048]{2,1,0:T(8,128)(2,1)} custom-call(s32[4]{0:T(128)} %fusion.20.blk_ref, bf16[2048,2048]{1,0:T(8,128)(2,1)} %get-tuple-element.122.l0_ref.l1_ref, bf16[2048,2048]{1,0:T(8,128)(2,1)} %get-tuple-element.122.l0_ref.l1_ref, bf16[2048,2048]{1,0:T(8,128)(2,1)} %get-tuple-element.123.r_ref, bf16[4,256,2048]{2,1,0:T(8,128)(2,1)} %collective-permute-done.14.refs_0_), custom_call_target="tpu_custom_call" | custom-call | flops 8589934592 | bytes 20971520 | tf_op jit(solution)/shard_map/dw/pallas_call | solution.py:535
  717.1 18.1 %dw.16 = bf16[4,256,2048]{2,1,0:T(8,128)(2,1)} custom-call(s32[4]{0:T(128)} %fusion.20.blk_ref, bf16[2048,2048]{1,0:T(8,128)(2,1)} %get-tuple-element.119.l0_ref.l1_ref, bf16[2048,2048]{1,0:T(8,128)(2,1)} %get-tuple-element.119.l0_ref.l1_ref, bf16[2048,2048]{1,0:T(8,128)(2,1)} %get-tuple-element.121.r_ref, bf16[4,256,2048]{2,1,0:T(8,128)(2,1)} %collective-permute-done.13.refs_0_), custom_call_target="tpu_custom_call" | custom-call | flops 8589934592 | bytes 20971520 | tf_op jit(solution)/shard_map/dw/pallas_call | solution.py:535
  735.3 18.2 %dw.15 = bf16[4,256,2048]{2,1,0:T(8,128)(2,1)} custom-call(s32[4]{0:T(128)} %fusion.20.blk_ref, bf16[2048,2048]{1,0:T(8,128)(2,1)} %get-tuple-element.119.l0_ref.l1_ref, bf16[2048,2048]{1,0:T(8,128)(2,1)} %get-tuple-element.119.l0_ref.l1_ref, bf16[2048,2048]{1,0:T(8,128)(2,1)} %get-tuple-element.120.r_ref, bf16[4,256,2048]{2,1,0:T(8,128)(2,1)} %collective-permute-done.12.refs_0_), custom_call_target="tpu_custom_call" | custom-call | flops 8589934592 | bytes 20971520 | tf_op jit(solution)/shard_map/dw/pallas_call | solution.py:535
  761.1 3.4 fusion.23
  764.5 7.7 dw.18
  775.3 9.1 d_o.1.do_ref
  784.4 13.8 %attend_back.4 = (f32[16,128,512]{2,1,0:T(8,128)}, bf16[512,1024]{1,0:T(8,128)(2,1)}) custom-call(s32[1]{0:T(128)} %bitcast.1.info_ref, bf16[512,2048]{1,0:T(8,128)(2,1)} %get-tuple-element.90.q_ref, bf16[512,2048]{1,0:T(8,128)(2,1)} %d_o.1.do_ref, bf16[512,2048]{1,0:T(8,128)(2,1)} %get-tuple-element.94.o_ref.r_ref, ...), custom_call_target="tpu_custom_call" | custom-call | flops 5368709120 | bytes 12582912 | tf_op jit(solution)/shard_map/attend_back/pallas_call | solution.py:285
  798.2 8.5 dw.19
  809.9 5.1 collective-permute-start.18
  816.0 15.3 %collective-permute-start.17 = (bf16[2,256,1024]{2,1,0:T(8,128)(2,1)}, bf16[2,256,1024]{2,1,0:T(8,128)(2,1)}, u32[]{:S(2)}, u32[]{:S(2)}) collective-permute-start(bf16[2,256,1024]{2,1,0:T(8,128)(2,1)} %slice_bitcast_fusion.2), channel_id=1, source_target_pairs={{0,8},{4,12},{8,0},{12,4},{16,24},{20,28},{24,16},{28,20},{1,9},{5... | collective-permute-start | bytes 3145736 | tf_op jit(solution)/shard_map/ppermute | solution.py:735
  831.3 3.7 add_convert_fusion.2
  836.6 14.6 %attend_back.5 = (f32[16,128,512]{2,1,0:T(8,128)}, bf16[512,1024]{1,0:T(8,128)(2,1)}) custom-call(s32[1]{0:T(128)} %bitcast.1.info_ref, bf16[512,2048]{1,0:T(8,128)(2,1)} %get-tuple-element.90.q_ref, bf16[512,2048]{1,0:T(8,128)(2,1)} %d_o.1.do_ref, bf16[512,2048]{1,0:T(8,128)(2,1)} %get-tuple-element.94.o_ref.r_ref, ...), custom_call_target="tpu_custom_call" | custom-call | flops 5368709120 | bytes 12582912 | tf_op jit(solution)/shard_map/attend_back/pallas_call | solution.py:285
  853.3 12.0 collective-permute-done.17
  879.1 14.3 %attend_back.6 = (f32[16,128,512]{2,1,0:T(8,128)}, bf16[512,1024]{1,0:T(8,128)(2,1)}) custom-call(s32[1]{0:T(128)} %bitcast.1.info_ref, bf16[512,2048]{1,0:T(8,128)(2,1)} %get-tuple-element.90.q_ref, bf16[512,2048]{1,0:T(8,128)(2,1)} %d_o.1.do_ref, bf16[512,2048]{1,0:T(8,128)(2,1)} %get-tuple-element.94.o_ref.r_ref, ...), custom_call_target="tpu_custom_call" | custom-call | flops 5368709120 | bytes 12582912 | tf_op jit(solution)/shard_map/attend_back/pallas_call | solution.py:285
  896.7 56.1 %collective-permute-done.20 = bf16[512,1024]{1,0:T(8,128)(2,1)} collective-permute-done((bf16[512,1024]{1,0:T(8,128)(2,1)S(1)}, bf16[512,1024]{1,0:T(8,128)(2,1)}, u32[]{:S(2)}, u32[]{:S(2)}) %collective-permute-start.20) | collective-permute-done | bytes 1048608 | tf_op jit(solution)/shard_map/ppermute | solution.py:758
  957.2 33.3 %attend_back.7 = (bf16[512,2048]{1,0:T(8,128)(2,1)}, bf16[512,1024]{1,0:T(8,128)(2,1)}) custom-call(s32[1]{0:T(128)} %bitcast.1.info_ref, bf16[512,2048]{1,0:T(8,128)(2,1)} %get-tuple-element.90.q_ref, bf16[512,2048]{1,0:T(8,128)(2,1)} %d_o.1.do_ref, bf16[512,2048]{1,0:T(8,128)(2,1)} %get-tuple-element.94.o_ref.r_ref, ...), custom_call_target="tpu_custom_call" | custom-call | flops 5368709120 | bytes 12582912 | tf_op jit(solution)/shard_map/attend_back/pallas_call | solution.py:285
  990.4 3.8 add_convert_fusion.1
  994.2 7.7 dw.20
  1002.2 4.1 unturn.1.dkv_ref.r_ref
  1006.3 4.7 dw.22
  1012.2 3.5 collective-permute-done.36.refs_0_
  1015.7 5.0 dw.23
  1025.2 13.6 %d_n1.1 = f32[512,2048]{1,0:T(8,128)} custom-call(bf16[512,2048]{1,0:T(8,128)(2,1)} %get-tuple-element.159.dq_ref.r_ref, bf16[512,1024]{1,0:T(8,128)(2,1)} %unturn.1.dkv_ref.r_ref, bf16[8,4,256,768]{3,2,1,0:T(8,128)(2,1)} %bitcast.122), custom_call_target="tpu_custom_call" | custom-call | flops 6442450944 | bytes 16777216 | tf_op jit(solution)/shard_map/d_n1/pallas_call | solution.py:496
  1039.6 4.1 collective-permute-start.39
  1043.7 8.7 dw.21
  1062.5 4.9 collective-permute-done.38
  1067.4 27.2 %collective-permute-done.32 = bf16[2,256,1024]{2,1,0:T(8,128)(2,1)S(1)} collective-permute-done((bf16[2,256,1024]{2,1,0:T(8,128)(2,1)S(1)}, bf16[2,256,1024]{2,1,0:T(8,128)(2,1)S(1)}, u32[]{:S(2)}, u32[]{:S(2)}) %collective-permute-start.32) | collective-permute-done | bytes 1048608 | tf_op jit(solution)/shard_map/ppermute | solution.py:735
  1097.3 3.7 collective-permute-done.34
  1105.8 6.1 collective-permute-done.33
  1118.2 3.2 pad_maximum_fusion
  1121.4 3.6 fusion.9
  1125.1 9.9 collective-permute-start.26
  1136.7 4.4 collective-permute-start.27
  1141.1 3.3 collective-permute-done.27
  1151.1 4.7 fusion.6
  1162.5 2.9 bitcast_convert_fusion.1
  1165.4 63.8 %collective-permute-done.24 = bf16[512,2048]{1,0:T(8,128)(2,1)} collective-permute-done((bf16[512,2048]{1,0:T(8,128)(2,1)}, bf16[512,2048]{1,0:T(8,128)(2,1)}, u32[]{:S(2)}, u32[]{:S(2)}) %collective-permute-start.24) | collective-permute-done | bytes 2097184 | tf_op jit(solution)/shard_map/ppermute | solution.py:707
  1229.2 5.4 add_convert_fusion
  (206 shorter events, 120.3 us)
Async XLA Ops:
  7.2 166.8 %all-gather.5.cloned.1.call-start = ((), (), s32[]{:S(2)}) async-start(), calls=%async_computation.5 | async-start | bytes 12976128 | tf_op jit(solution)/shard_map/all_gather | solution.py:632
  8.8 70.7 %copy-start.3 = (bf16[512,2048]{1,0:T(8,128)(2,1)S(1)}, bf16[512,2048]{1,0:T(8,128)(2,1)}, u32[]{:S(2)}) copy-start(bf16[512,2048]{1,0:T(8,128)(2,1)} %x_ref.1) | copy-start | bytes 6291460
  10.7 308.7 %all-gather.7.cloned.1.call-start = ((), (), s32[]{:S(2)}) async-start(), calls=%async_computation.6 | async-start | bytes 8650752 | tf_op jit(solution)/shard_map/all_gather | solution.py:635
  12.4 1144.0 %reduce-scatter.17.cloned.1.call-start = ((), (), s32[]{:S(2)}) async-start(), calls=%async_computation.9 | async-start | bytes 5242880
  12.5 59.5 %collective-permute-start = (bf16[512,2048]{1,0:T(8,128)(2,1)}, bf16[512,2048]{1,0:T(8,128)(2,1)}, u32[]{:S(2)}, u32[]{:S(2)}) collective-permute-start(bf16[512,2048]{1,0:T(8,128)(2,1)} %g_ref), channel_id=1, source_target_pairs={{0,1},{1,2},{2,3},{3,0},{4,5},{5,6},{6,7},{7,4},{8,9},{9,10},{10,1... | collective-permute-start | bytes 6291464 | tf_op jit(solution)/shard_map/ppermute | solution.py:649
  72.0 83.5 %collective-permute-start.1 = (bf16[512,2048]{1,0:T(8,128)(2,1)}, bf16[512,2048]{1,0:T(8,128)(2,1)}, u32[]{:S(2)}, u32[]{:S(2)}) collective-permute-start(bf16[512,2048]{1,0:T(8,128)(2,1)} %collective-permute-done.g_ref), channel_id=1, source_target_pairs={{0,1},{1,2},{2,3},{3,0},{4,5},{5,6},{6,7},{7,4},{8,9},{9,10},{10,1... | collective-permute-start | bytes 6291464 | tf_op jit(solution)/shard_map/ppermute | solution.py:649
  72.8 113.3 %copy-start.19 = (f32[2048]{0:T(1024)}, f32[2048]{0:T(1024)S(1)}, u32[]{:S(2)}) copy-start(f32[2048]{0:T(1024)S(1)} %convert_element_type.259) | copy-start | bytes 24580
  174.0 108.3 %copy-start.25 = (bf16[2048]{0:T(1024)(128)(2,1)S(1)}, bf16[2048]{0:T(1024)(128)(2,1)}, u32[]{:S(2)}) copy-start(bf16[2048]{0:T(1024)(128)(2,1)} %param.20) | copy-start | bytes 12292
  186.1 39.4 %collective-permute-start.2 = (bf16[512,1024]{1,0:T(8,128)(2,1)}, bf16[512,1024]{1,0:T(8,128)(2,1)S(1)}, u32[]{:S(2)}, u32[]{:S(2)}) collective-permute-start(bf16[512,1024]{1,0:T(8,128)(2,1)} %get-tuple-element.91.refs_0_), channel_id=1, source_target_pairs={{0,1},{1,2},{2,3},{4,5},{5,6},{6,7},{8,9},{9,10},{10,11},{12,13},{... | collective-permute-start | bytes 3145736 | tf_op jit(solution)/shard_map/ppermute | solution.py:661
  225.6 73.6 %copy-start.26 = (bf16[512,1024]{1,0:T(8,128)(2,1)}, bf16[512,1024]{1,0:T(8,128)(2,1)S(1)}, u32[]{:S(2)}) copy-start(bf16[512,1024]{1,0:T(8,128)(2,1)S(1)} %collective-permute-done.2.refs_1_.refs_0_) | copy-start | bytes 3145732
  225.6 47.6 %collective-permute-start.3 = (bf16[512,1024]{1,0:T(8,128)(2,1)S(1)}, bf16[512,1024]{1,0:T(8,128)(2,1)S(1)}, u32[]{:S(2)}, u32[]{:S(2)}) collective-permute-start(bf16[512,1024]{1,0:T(8,128)(2,1)S(1)} %collective-permute-done.2.refs_1_.refs_0_), channel_id=1, source_target_pairs={{0,1},{1,2},{2,3},{4,5},{5,6},{6,7},{8,9},{9,10},{10,11},{12,13},{... | collective-permute-start | bytes 3145736 | tf_op jit(solution)/shard_map/ppermute | solution.py:661
  273.2 26.0 %copy-start.27 = (bf16[512,1024]{1,0:T(8,128)(2,1)}, bf16[512,1024]{1,0:T(8,128)(2,1)S(1)}, u32[]{:S(2)}) copy-start(bf16[512,1024]{1,0:T(8,128)(2,1)S(1)} %collective-permute-done.3.refs_2_.refs_0_) | copy-start | bytes 3145732
  273.2 26.0 %collective-permute-start.4 = (bf16[512,1024]{1,0:T(8,128)(2,1)S(1)}, bf16[512,1024]{1,0:T(8,128)(2,1)}, u32[]{:S(2)}, u32[]{:S(2)}) collective-permute-start(bf16[512,1024]{1,0:T(8,128)(2,1)S(1)} %collective-permute-done.3.refs_2_.refs_0_), channel_id=1, source_target_pairs={{0,1},{1,2},{2,3},{4,5},{5,6},{6,7},{8,9},{9,10},{10,11},{12,13},{... | collective-permute-start | bytes 3145736 | tf_op jit(solution)/shard_map/ppermute | solution.py:661
  333.2 66.8 %collective-permute-start.5 = (bf16[512,2048]{1,0:T(8,128)(2,1)}, bf16[512,2048]{1,0:T(8,128)(2,1)}, u32[]{:S(2)}, u32[]{:S(2)}) collective-permute-start(bf16[512,2048]{1,0:T(8,128)(2,1)} %get-tuple-element.96.n2_ref), channel_id=1, source_target_pairs={{0,1},{1,2},{2,3},{3,0},{4,5},{5,6},{6,7},{7,4},{8,9},{9,10},{10,1... | collective-permute-start | bytes 6291464 | tf_op jit(solution)/shard_map/ppermute | solution.py:670
  353.6 225.7 %collective-permute-start.10 = (bf16[512,2048]{1,0:T(8,128)(2,1)}, bf16[512,2048]{1,0:T(8,128)(2,1)}, u32[]{:S(2)}, u32[]{:S(2)}) collective-permute-start(bf16[512,2048]{1,0:T(8,128)(2,1)} %collective-permute-done.1.g_ref), channel_id=1, source_target_pairs={{0,1},{1,2},{2,3},{3,0},{4,5},{5,6},{6,7},{7,4},{8,9},{9,10},{10,1... | collective-permute-start | bytes 6291464 | tf_op jit(solution)/shard_map/ppermute | solution.py:663
  400.0 89.9 %collective-permute-start.6 = (bf16[512,2048]{1,0:T(8,128)(2,1)}, bf16[512,2048]{1,0:T(8,128)(2,1)}, u32[]{:S(2)}, u32[]{:S(2)}) collective-permute-start(bf16[512,2048]{1,0:T(8,128)(2,1)} %collective-permute-done.5.n2_ref), channel_id=1, source_target_pairs={{0,1},{1,2},{2,3},{3,0},{4,5},{5,6},{6,7},{7,4},{8,9},{9,10},{10,1... | collective-permute-start | bytes 6291464 | tf_op jit(solution)/shard_map/ppermute | solution.py:670
  444.4 90.4 %collective-permute-start.8 = (bf16[512,2048]{1,0:T(8,128)(2,1)}, bf16[512,2048]{1,0:T(8,128)(2,1)S(1)}, u32[]{:S(2)}, u32[]{:S(2)}) collective-permute-start(bf16[512,2048]{1,0:T(8,128)(2,1)} %get-tuple-element.104), channel_id=1, source_target_pairs={{0,1},{1,2},{2,3},{3,0},{4,5},{5,6},{6,7},{7,4},{8,9},{9,10},{10,1... | collective-permute-start | bytes 6291464 | tf_op jit(solution)/shard_map/ppermute | solution.py:684
  489.9 86.9 %collective-permute-start.7 = (bf16[512,2048]{1,0:T(8,128)(2,1)}, bf16[512,2048]{1,0:T(8,128)(2,1)}, u32[]{:S(2)}, u32[]{:S(2)}) collective-permute-start(bf16[512,2048]{1,0:T(8,128)(2,1)} %collective-permute-done.6.n2_ref), channel_id=1, source_target_pairs={{0,1},{1,2},{2,3},{3,0},{4,5},{5,6},{6,7},{7,4},{8,9},{9,10},{10,1... | collective-permute-start | bytes 6291464 | tf_op jit(solution)/shard_map/ppermute | solution.py:670
  576.7 97.2 %collective-permute-start.9 = (bf16[512,2048]{1,0:T(8,128)(2,1)}, bf16[512,2048]{1,0:T(8,128)(2,1)S(1)}, u32[]{:S(2)}, u32[]{:S(2)}) collective-permute-start(bf16[512,2048]{1,0:T(8,128)(2,1)} %add_convert_fusion.4), channel_id=1, source_target_pairs={{0,1},{1,2},{2,3},{3,0},{4,5},{5,6},{6,7},{7,4},{8,9},{9,10},{10,1... | collective-permute-start | bytes 6291464 | tf_op jit(solution)/shard_map/ppermute | solution.py:692
  674.0 25.0 %collective-permute-start.14 = (bf16[4,256,2048]{2,1,0:T(8,128)(2,1)}, bf16[4,256,2048]{2,1,0:T(8,128)(2,1)}, u32[]{:S(2)}, u32[]{:S(2)}) collective-permute-start(bf16[4,256,2048]{2,1,0:T(8,128)(2,1)} %dw.14), channel_id=1, source_target_pairs={{0,4},{4,0},{8,12},{12,8},{16,20},{20,16},{24,28},{28,24},{1,5},{5... | collective-permute-start | bytes 12582920 | tf_op jit(solution)/shard_map/ppermute | solution.py:696
  676.7 40.4 %collective-permute-start.13 = (bf16[4,256,2048]{2,1,0:T(8,128)(2,1)}, bf16[4,256,2048]{2,1,0:T(8,128)(2,1)}, u32[]{:S(2)}, u32[]{:S(2)}) collective-permute-start(bf16[4,256,2048]{2,1,0:T(8,128)(2,1)} %dw.13), channel_id=1, source_target_pairs={{0,4},{4,0},{8,12},{12,8},{16,20},{20,16},{24,28},{28,24},{1,5},{5... | collective-permute-start | bytes 12582920 | tf_op jit(solution)/shard_map/ppermute | solution.py:696
  676.8 58.5 %collective-permute-start.12 = (bf16[4,256,2048]{2,1,0:T(8,128)(2,1)}, bf16[4,256,2048]{2,1,0:T(8,128)(2,1)}, u32[]{:S(2)}, u32[]{:S(2)}) collective-permute-start(bf16[4,256,2048]{2,1,0:T(8,128)(2,1)} %dw.12), channel_id=1, source_target_pairs={{0,4},{4,0},{8,12},{12,8},{16,20},{20,16},{24,28},{28,24},{1,5},{5... | collective-permute-start | bytes 12582920 | tf_op jit(solution)/shard_map/ppermute | solution.py:696
  681.5 72.0 %collective-permute-start.11 = (bf16[512,2048]{1,0:T(8,128)(2,1)}, bf16[512,2048]{1,0:T(8,128)(2,1)}, u32[]{:S(2)}, u32[]{:S(2)}) collective-permute-start(bf16[512,2048]{1,0:T(8,128)(2,1)} %add_convert_fusion.3), channel_id=1, source_target_pairs={{0,1},{1,2},{2,3},{3,0},{4,5},{5,6},{6,7},{7,4},{8,9},{9,10},{10,1... | collective-permute-start | bytes 6291464 | tf_op jit(solution)/shard_map/ppermute | solution.py:695
  753.5 406.1 %reduce-scatter.15.cloned.1.call-start = ((), (), s32[]{:S(2)}) async-start(), calls=%async_computation.8 | async-start | bytes 5242880
  772.2 26.0 %collective-permute-start.15 = (bf16[4,256,2048]{2,1,0:T(8,128)(2,1)}, bf16[4,256,2048]{2,1,0:T(8,128)(2,1)}, u32[]{:S(2)}, u32[]{:S(2)}) collective-permute-start(bf16[4,256,2048]{2,1,0:T(8,128)(2,1)} %dw.18), channel_id=1, source_target_pairs={{0,4},{4,0},{8,12},{12,8},{16,20},{20,16},{24,28},{28,24},{1,5},{5... | collective-permute-start | bytes 12582920 | tf_op jit(solution)/shard_map/ppermute | solution.py:719
  772.2 390.2 %reduce-scatter.13.cloned.1.call-start = ((), (), s32[]{:S(2)}) async-start(), calls=%async_computation.7 | async-start | bytes 5242880
  772.3 59.0 %collective-permute-start.19 = (bf16[512,2048]{1,0:T(8,128)(2,1)}, bf16[512,2048]{1,0:T(8,128)(2,1)}, u32[]{:S(2)}, u32[]{:S(2)}) collective-permute-start(bf16[512,2048]{1,0:T(8,128)(2,1)} %get-tuple-element.144), channel_id=1, source_target_pairs={{0,1},{1,2},{2,3},{3,0},{4,5},{5,6},{6,7},{7,4},{8,9},{9,10},{10,1... | collective-permute-start | bytes 6291464 | tf_op jit(solution)/shard_map/ppermute | solution.py:705
  806.7 24.6 %copy-start.15 = (bf16[512,2048]{1,0:T(8,128)(2,1)S(1)}, bf16[512,2048]{1,0:T(8,128)(2,1)}, u32[]{:S(2)}) copy-start(bf16[512,2048]{1,0:T(8,128)(2,1)} %get-tuple-element.145) | copy-start | bytes 6291460
  809.9 41.3 %collective-permute-start.18 = (bf16[2,256,1024]{2,1,0:T(8,128)(2,1)S(1)}, bf16[2,256,1024]{2,1,0:T(8,128)(2,1)}, u32[]{:S(2)}, u32[]{:S(2)}) collective-permute-start(bf16[2,256,1024]{2,1,0:T(8,128)(2,1)S(1)} %slice.122), channel_id=1, source_target_pairs={{0,16},{4,20},{8,24},{12,28},{16,0},{20,4},{24,8},{28,12},{1,17},{... | collective-permute-start | bytes 3145736 | tf_op jit(solution)/shard_map/ppermute | solution.py:735
  816.0 49.3 %collective-permute-start.17 = (bf16[2,256,1024]{2,1,0:T(8,128)(2,1)}, bf16[2,256,1024]{2,1,0:T(8,128)(2,1)}, u32[]{:S(2)}, u32[]{:S(2)}) collective-permute-start(bf16[2,256,1024]{2,1,0:T(8,128)(2,1)} %slice_bitcast_fusion.2), channel_id=1, source_target_pairs={{0,8},{4,12},{8,0},{12,4},{16,24},{20,28},{24,16},{28,20},{1,9},{5... | collective-permute-start | bytes 3145736 | tf_op jit(solution)/shard_map/ppermute | solution.py:735
  834.9 32.0 %collective-permute-start.16 = (bf16[512,1024]{1,0:T(8,128)(2,1)}, bf16[512,1024]{1,0:T(8,128)(2,1)}, u32[]{:S(2)}, u32[]{:S(2)}) collective-permute-start(bf16[512,1024]{1,0:T(8,128)(2,1)} %get-tuple-element.141), channel_id=1, source_target_pairs={{1,0},{2,1},{3,2},{5,4},{6,5},{7,6},{9,8},{10,9},{11,10},{13,12},{... | collective-permute-start | bytes 3145736 | tf_op jit(solution)/shard_map/ppermute | solution.py:758
  851.2 15.7 %copy-start.18 = (bf16[512,1024]{1,0:T(8,128)(2,1)S(1)}, bf16[512,1024]{1,0:T(8,128)(2,1)}, u32[]{:S(2)}) copy-start(bf16[512,1024]{1,0:T(8,128)(2,1)} %get-tuple-element.142) | copy-start | bytes 3145732
  866.9 8.7 copy-start.8
  869.1 121.4 %collective-permute-start.23 = (bf16[512,2048]{1,0:T(8,128)(2,1)}, bf16[512,2048]{1,0:T(8,128)(2,1)}, u32[]{:S(2)}, u32[]{:S(2)}) collective-permute-start(bf16[512,2048]{1,0:T(8,128)(2,1)} %add_convert_fusion.2), channel_id=1, source_target_pairs={{0,1},{1,2},{2,3},{3,0},{4,5},{5,6},{6,7},{7,4},{8,9},{9,10},{10,1... | collective-permute-start | bytes 6291464 | tf_op jit(solution)/shard_map/ppermute | solution.py:705
  871.7 21.7 %collective-permute-start.22 = (bf16[256,1024]{1,0:T(8,128)(2,1)S(1)}, bf16[256,1024]{1,0:T(8,128)(2,1)}, u32[]{:S(2)}, u32[]{:S(2)}) collective-permute-start(bf16[256,1024]{1,0:T(8,128)(2,1)S(1)} %slice_bitcast_fusion.11), channel_id=1, source_target_pairs={{0,8},{4,12},{8,0},{12,4},{16,24},{20,28},{24,16},{28,20},{1,9},{5... | collective-permute-start | bytes 1572872 | tf_op jit(solution)/shard_map/ppermute | solution.py:735
  874.4 78.5 %collective-permute-start.20 = (bf16[512,1024]{1,0:T(8,128)(2,1)S(1)}, bf16[512,1024]{1,0:T(8,128)(2,1)}, u32[]{:S(2)}, u32[]{:S(2)}) collective-permute-start(bf16[512,1024]{1,0:T(8,128)(2,1)S(1)} %add_convert_fusion.8), channel_id=1, source_target_pairs={{1,0},{2,1},{3,2},{5,4},{6,5},{7,6},{9,8},{10,9},{11,10},{13,12},{... | collective-permute-start | bytes 3145736 | tf_op jit(solution)/shard_map/ppermute | solution.py:758
  876.5 18.2 %copy-start.9 = (bf16[2,256,1024]{2,1,0:T(8,128)(2,1)S(1)}, bf16[2,256,1024]{2,1,0:T(8,128)(2,1)}, u32[]{:S(2)}) copy-start(bf16[2,256,1024]{2,1,0:T(8,128)(2,1)} %copy-done.8) | copy-start | bytes 3145732
  876.5 18.2 %collective-permute-start.21 = (bf16[256,1024]{1,0:T(8,128)(2,1)}, bf16[256,1024]{1,0:T(8,128)(2,1)}, u32[]{:S(2)}, u32[]{:S(2)}) collective-permute-start(bf16[256,1024]{1,0:T(8,128)(2,1)} %slice_bitcast_fusion.12), channel_id=1, source_target_pairs={{0,16},{4,20},{8,24},{12,28},{16,0},{20,4},{24,8},{28,12},{1,17},{... | collective-permute-start | bytes 1572872 | tf_op jit(solution)/shard_map/ppermute | solution.py:735
  955.7 34.7 %copy-start.14 = (bf16[512,2048]{1,0:T(8,128)(2,1)S(1)}, bf16[512,2048]{1,0:T(8,128)(2,1)}, u32[]{:S(2)}) copy-start(bf16[512,2048]{1,0:T(8,128)(2,1)} %get-tuple-element.156) | copy-start | bytes 6291460
  955.8 46.5 %collective-permute-start.25 = (bf16[512,1024]{1,0:T(8,128)(2,1)}, bf16[512,1024]{1,0:T(8,128)(2,1)}, u32[]{:S(2)}, u32[]{:S(2)}) collective-permute-start(bf16[512,1024]{1,0:T(8,128)(2,1)} %add_convert_fusion.6), channel_id=1, source_target_pairs={{1,0},{2,1},{3,2},{5,4},{6,5},{7,6},{9,8},{10,9},{11,10},{13,12},{... | collective-permute-start | bytes 3145736 | tf_op jit(solution)/shard_map/ppermute | solution.py:764
  1002.0 41.8 %collective-permute-start.31 = (bf16[4,256,2048]{2,1,0:T(8,128)(2,1)}, bf16[4,256,2048]{2,1,0:T(8,128)(2,1)}, u32[]{:S(2)}, u32[]{:S(2)}) collective-permute-start(bf16[4,256,2048]{2,1,0:T(8,128)(2,1)} %dw.20), channel_id=1, source_target_pairs={{0,4},{4,0},{8,12},{12,8},{16,20},{20,16},{24,28},{28,24},{1,5},{5... | collective-permute-start | bytes 12582920 | tf_op jit(solution)/shard_map/ppermute | solution.py:719
  1002.0 232.7 %reduce-scatter.11.cloned.1.call-start = ((), (), s32[]{:S(2)}) async-start(), calls=%async_computation.4 | async-start | bytes 3276800 | tf_op jit(solution)/shard_map/reduce_scatter | solution.py:784
  1006.3 5.2 copy-start.16
  1011.0 4.6 collective-permute-start.36
  1023.8 15.0 %copy-start.7 = (bf16[4,256,1024]{2,1,0:T(8,128)(2,1)S(1)}, bf16[4,256,1024]{2,1,0:T(8,128)(2,1)}, u32[]{:S(2)}) copy-start(bf16[4,256,1024]{2,1,0:T(8,128)(2,1)} %dw.23) | copy-start | bytes 6291460
  1023.8 32.5 %collective-permute-start.37 = (bf16[2,256,512]{2,1,0:T(8,128)(2,1)}, bf16[2,256,512]{2,1,0:T(8,128)(2,1)}, u32[]{:S(2)}, u32[]{:S(2)}) collective-permute-start(bf16[2,256,512]{2,1,0:T(8,128)(2,1)} %slice_bitcast_fusion.5), channel_id=1, source_target_pairs={{0,8},{4,12},{8,0},{12,4},{16,24},{20,28},{24,16},{28,20},{1,9},{5... | collective-permute-start | bytes 1572872 | tf_op jit(solution)/shard_map/ppermute | solution.py:735
  1039.6 22.3 %collective-permute-start.39 = (bf16[2,256,512]{2,1,0:T(8,128)(2,1)}, bf16[2,256,512]{2,1,0:T(8,128)(2,1)S(1)}, u32[]{:S(2)}, u32[]{:S(2)}) collective-permute-start(bf16[2,256,512]{2,1,0:T(8,128)(2,1)} %slice.169), channel_id=1, source_target_pairs={{0,16},{4,20},{8,24},{12,28},{16,0},{20,4},{24,8},{28,12},{1,17},{... | collective-permute-start | bytes 1572872 | tf_op jit(solution)/shard_map/ppermute | solution.py:735
  1052.5 5.1 copy-start.6
  1054.5 40.1 %collective-permute-start.32 = (bf16[2,256,1024]{2,1,0:T(8,128)(2,1)S(1)}, bf16[2,256,1024]{2,1,0:T(8,128)(2,1)S(1)}, u32[]{:S(2)}, u32[]{:S(2)}) collective-permute-start(bf16[2,256,1024]{2,1,0:T(8,128)(2,1)S(1)} %slice_bitcast_fusion), channel_id=1, source_target_pairs={{0,8},{4,12},{8,0},{12,4},{16,24},{20,28},{24,16},{28,20},{1,9},{5... | collective-permute-start | bytes 3145736 | tf_op jit(solution)/shard_map/ppermute | solution.py:735
  1057.5 9.9 collective-permute-start.38
  1057.7 43.4 %collective-permute-start.34 = (bf16[2,256,1024]{2,1,0:T(8,128)(2,1)S(1)}, bf16[2,256,1024]{2,1,0:T(8,128)(2,1)S(1)}, u32[]{:S(2)}, u32[]{:S(2)}) collective-permute-start(bf16[2,256,1024]{2,1,0:T(8,128)(2,1)S(1)} %slice.160), channel_id=1, source_target_pairs={{0,16},{4,20},{8,24},{12,28},{16,0},{20,4},{24,8},{28,12},{1,17},{... | collective-permute-start | bytes 3145736 | tf_op jit(solution)/shard_map/ppermute | solution.py:735
  1062.1 40.8 %collective-permute-start.40 = (bf16[256,512]{1,0:T(8,128)(2,1)S(1)}, bf16[256,512]{1,0:T(8,128)(2,1)S(1)}, u32[]{:S(2)}, u32[]{:S(2)}) collective-permute-start(bf16[256,512]{1,0:T(8,128)(2,1)S(1)} %slice_bitcast_fusion.13), channel_id=1, source_target_pairs={{0,8},{4,12},{8,0},{12,4},{16,24},{20,28},{24,16},{28,20},{1,9},{5... | collective-permute-start | bytes 786440 | tf_op jit(solution)/shard_map/ppermute | solution.py:735
  1095.8 16.1 %collective-permute-start.33 = (bf16[256,1024]{1,0:T(8,128)(2,1)}, bf16[256,1024]{1,0:T(8,128)(2,1)}, u32[]{:S(2)}, u32[]{:S(2)}) collective-permute-start(bf16[256,1024]{1,0:T(8,128)(2,1)} %slice_bitcast_fusion.9), channel_id=1, source_target_pairs={{0,16},{4,20},{8,24},{12,28},{16,0},{20,4},{24,8},{28,12},{1,17},{... | collective-permute-start | bytes 1572872 | tf_op jit(solution)/shard_map/ppermute | solution.py:735
  1102.3 13.2 %collective-permute-start.35 = (bf16[256,1024]{1,0:T(8,128)(2,1)}, bf16[256,1024]{1,0:T(8,128)(2,1)}, u32[]{:S(2)}, u32[]{:S(2)}) collective-permute-start(bf16[256,1024]{1,0:T(8,128)(2,1)} %slice_bitcast_fusion.7), channel_id=1, source_target_pairs={{0,8},{4,12},{8,0},{12,4},{16,24},{20,28},{24,16},{28,20},{1,9},{5... | collective-permute-start | bytes 1572872 | tf_op jit(solution)/shard_map/ppermute | solution.py:735
  1121.4 29.7 %copy-start.24 = (f32[512]{0:T(512)S(1)}, f32[512]{0:T(512)}, u32[]{:S(2)}) copy-start(f32[512]{0:T(512)} %get-tuple-element.225) | copy-start | bytes 6148
  1121.4 29.6 %copy-start.5 = (f32[512,2048]{1,0:T(8,128)S(1)}, f32[512,2048]{1,0:T(8,128)}, u32[]{:S(2)}) copy-start(f32[512,2048]{1,0:T(8,128)} %get-tuple-element.216) | copy-start | bytes 12582916
  1125.1 11.6 collective-permute-start.26
  1136.7 7.7 collective-permute-start.27
  1144.4 1.2 collective-permute-start.28
  1145.7 3.8 collective-permute-start.29
  1147.2 82.0 %collective-permute-start.24 = (bf16[512,2048]{1,0:T(8,128)(2,1)}, bf16[512,2048]{1,0:T(8,128)(2,1)}, u32[]{:S(2)}, u32[]{:S(2)}) collective-permute-start(bf16[512,2048]{1,0:T(8,128)(2,1)} %add_convert_fusion.1), channel_id=1, source_target_pairs={{0,1},{1,2},{2,3},{3,0},{4,5},{5,6},{6,7},{7,4},{8,9},{9,10},{10,1... | collective-permute-start | bytes 6291464 | tf_op jit(solution)/shard_map/ppermute | solution.py:707
  1149.5 6.2 collective-permute-start.30
  1162.4 66.8 %copy-start.13 = (bf16[512,2048]{1,0:T(8,128)(2,1)S(1)}, bf16[512,2048]{1,0:T(8,128)(2,1)}, u32[]{:S(2)}) copy-start(bf16[512,2048]{1,0:T(8,128)(2,1)} %get-tuple-element.158) | copy-start | bytes 6291460
  1229.2 10.0 copy-start.1
  (11 other events, 30.1 us)
Sparse Core Ops, SparseCore 0:
  11.5 162.4 all-gather.4
  177.5 96.7 all-gather.6
  753.7 82.1 reduce-scatter.16
  838.7 72.6 reduce-scatter.14
  1002.1 93.6 reduce-scatter.12
  1121.5 92.8 reduce-scatter.10
